TPU v7x, 256 devices: a whole 4x4x8 slice. The times are simulated.
256 devices in a mesh: energy: 64 (over z, x, core), atom: 4 (over y).
Axes of the slice: x: 4, y: 4, z: 8, core: 2. Of those that a mesh axis runs over, the one named last changes fastest.
Arguments:
- green_blocks: float32 [256, 32, 34, 288], P('energy', 'atom'), may hold values from -6 to 6
- coupling: float32 [32, 12, 12], P('atom'), may hold values from -1.75 to 1.75
- neighbours: int32 [32, 34], P('atom'), may hold values from 0 to 31
- freq_offset: int32 [64], replicated, may hold values from 1 to 2, as said below
- emit_weight: float32 [64], replicated, may hold values from 0.02 to 0.2
- absorb_weight: float32 [64], replicated, may hold values from 0.02 to 0.2
Outputs:
- sigma: float32 [256, 32, 34, 288], P('energy', 'atom')
Inputs may be any that keep to these rules, and one draw needn't show every extreme that they name: `freq_offset`: every offset is 1 or more and at least one offset equals 2.
All inputs are finite; a program needn't handle non-finite values.
Results may differ from a plain program's by a relative error of at most 0.00007.
Values sent between devices are 32-bit elements; how exact they have to be, the bound alone decides.
No kernel may reach another device: no remote copies, remote signals or barrier semaphores. Data moves between devices by JAX's collectives and lax.ppermute only.
A program may use at most 128 MiB of HBM per device.

v0:
```python
import jax
import jax.numpy as jnp
from jax import lax
from jax.experimental import pallas as pl
from jax.experimental.pallas import tpu as pltpu
from jax.sharding import PartitionSpec as P

OFF = 2
ROWS = 4
ORB = 12
NBR = 34
ATOM = 8
ROW = NBR * ATOM
WIDTH = 288
LANES = 128
TILES = 5
TAIL = 17
PACK = 4 * NBR + TAIL
F32 = jnp.float32
BF16 = jnp.bfloat16


def energy_of(row, core):
    return jnp.where(core == 0, row, ROWS - 1 - row)


def pack_kernel(green, coupling, outer, inner, flat, staged, sem):
    core = lax.axis_index("energy") % 2
    copies = []
    for row in range(2):
        copies.append(pltpu.make_async_copy(green.at[energy_of(row, core)], staged.at[pl.ds(NBR * row, NBR)], sem.at[row]))
    for row in range(2):
        copies.append(pltpu.make_async_copy(green.at[energy_of(3 - row, core)], inner.at[row], sem.at[2 + row]))
    for copy in copies:
        copy.start()
    pieces = [coupling[orbital] for orbital in range(ORB)] + [jnp.zeros((ATOM, 2 * LANES - ORB * ORB), F32)]
    flat[...] = jnp.concatenate(pieces, axis=-1)
    copies[0].wait()
    copies[1].wait()
    outer[0 : 2 * NBR] = staged[:, :, 0:128]
    outer[2 * NBR : 4 * NBR] = staged[:, :, 128:256]
    outer[4 * NBR : PACK] = jnp.concatenate([staged[TAIL * part : TAIL * (part + 1), :, 256:288] for part in range(4)], axis=-1)
    copies[2].wait()
    copies[3].wait()


def dress_tile(tile, natural, result, pair_coef, atom_coef, given, middle, turned):
    rows = pl.ds(pl.multiple_of(tile * LANES, LANES), LANES)
    x_ref, z_ref, y_ref = turned.at[0], middle, turned.at[1]
    x_ref[0:128] = natural[rows, 0:128].T
    x_ref[128:256] = natural[rows, 128:256].T
    x_ref[256:288] = natural[rows, 256:288].T
    low = lax.broadcasted_iota(jnp.int32, (8, LANES), 0) < 4
    x = [[[x_ref[pl.ds(144 * part + 24 * pair + 8 * k, 8)] for k in range(3)] for pair in range(6)] for part in range(2)]
    for a in range(ORB):
        totals = [[None] * 3 for _ in range(2)]
        for pair in range(6):
            first = jnp.broadcast_to(atom_coef[pl.ds(ORB * a + 2 * pair, 1)], (8, LANES))
            last = jnp.broadcast_to(atom_coef[pl.ds(ORB * a + 2 * pair + 1, 1)], (8, LANES))
            coef = (first, jnp.where(low, first, last), last)
            for part in range(2):
                for k in range(3):
                    term = coef[k] * x[part][pair][k]
                    totals[part][k] = term if pair == 0 else totals[part][k] + term
        for part in range(2):
            for k in range(3):
                z_ref[pl.ds((ORB * part + a) * 24 + 8 * k, 8)] = totals[part][k]
    z = []
    for d in range(ORB):
        z.append([z_ref[pl.ds(192 * k + d, 8, stride=24)] + z_ref[pl.ds(192 * k + 12 + d, 8, stride=24)] for k in range(3)])
    for f in range(ORB):
        totals = [None] * 3
        for d in range(ORB):
            coef = jnp.broadcast_to(pair_coef[tile, pl.ds(ORB * f + d, 1)], (8, LANES))
            for k in range(3):
                term = coef * z[d][k]
                totals[k] = term if d == 0 else totals[k] + term
        for k in range(3):
            y_ref[pl.ds(96 * k + f, 8, stride=ORB)] = totals[k]
    if given is not None:
        y_ref[...] = y_ref[...] + given[tile]
    if result is not None:
        result[rows, 0:128] = y_ref[0:128].T
        result[rows, 128:256] = y_ref[128:256].T
        result[rows, 256:288] = y_ref[256:288].T


def kernel_values(freq, emit, absorb, sign):
    sums = []
    for d in range(-OFF, OFF + 1):
        shift = d * sign
        terms = jnp.where(freq == -shift, emit, 0.0) + jnp.where(freq == shift, absorb, 0.0)
        sums.append(jnp.sum(terms, axis=1, keepdims=True))
    return sums


def local_kernel(green, near, flat, from_next, from_second, from_third, neighbours, freq, emit, absorb,
                 out, partial, pair_coef, atom_coef, outer_weights,
                 every, indices, natural, result, middle, turned, sem):
    position = lax.axis_index("energy")
    core = position % 2
    weights = kernel_values(freq[...], emit[...], absorb[...], 1 - 2 * core)
    inside = jnp.where((position > 0) & (position < lax.axis_size("energy") - 1), 1.0, 0.0).astype(F32)
    outer_weights[0] = jnp.broadcast_to(weights[1] * inside, (8, LANES))
    outer_weights[1] = jnp.broadcast_to(weights[0] * inside, (8, LANES))
    every[...] = jnp.zeros_like(every)
    for place, block in enumerate((flat, from_next, from_second, from_third)):
        every[8 * place : 8 * place + 8] = block[...]
    columns = every[...].T[0 : ORB * ORB]
    high = columns.astype(BF16)
    rest = columns - high.astype(F32)
    mid = rest.astype(BF16)
    low = (rest - mid.astype(F32)).astype(BF16)
    indices[...] = jnp.zeros_like(indices)
    indices[:, 0:NBR] = neighbours[...].astype(F32)
    width = TILES * LANES
    lane = lax.broadcasted_iota(jnp.int32, (LANES, width), 1)
    within = lane - jnp.where(lane >= ROW, ROW, 0) - jnp.where(lane >= 2 * ROW, ROW, 0)
    picks = (lax.shift_right_logical(within, 3) == lax.broadcasted_iota(jnp.int32, (LANES, width), 0)).astype(F32).astype(BF16)
    spread = jnp.dot(indices[...].astype(BF16), picks, preferred_element_type=F32)
    lane8 = lax.broadcasted_iota(jnp.int32, (ATOM, width), 1) & 7
    own = lane8 == lax.broadcasted_iota(jnp.int32, (ATOM, width), 0)
    listed = jnp.sum(jnp.where(own, spread, 0.0), axis=0, keepdims=True)
    listed = listed - (lax.axis_index("atom") * ATOM).astype(F32)
    listed = jnp.where(listed < 0, listed + 32.0, listed)
    number = lax.broadcasted_iota(jnp.int32, (LANES, width), 0).astype(F32)
    chosen = (number == listed).astype(F32).astype(BF16)
    spots = (lax.broadcasted_iota(jnp.int32, (LANES, LANES), 0) == (lax.broadcasted_iota(jnp.int32, (LANES, LANES), 1) & 7)).astype(F32).astype(BF16)

    def choose(hot):
        dot = lambda part: jnp.dot(part, hot, preferred_element_type=F32)
        return dot(high) + (dot(mid) + dot(low))

    for tile in range(TILES):
        pair_coef[tile] = choose(chosen[:, LANES * tile : LANES * (tile + 1)])
    atom_coef[...] = choose(spots)

    def rows_of(row):
        return green.at[energy_of(row, core)] if row < ROWS else near.at[row - ROWS]

    def energy_sum(base):
        def step(j, _):
            for half in range(2):
                row = base + half
                total = None
                for d in range(-OFF, OFF + 1):
                    if 0 <= row + d < ROWS + OFF:
                        term = weights[d + OFF] * rows_of(row + d)[j]
                        total = term if total is None else total + term
                natural[pl.ds(pl.multiple_of(ROW * half + 8 * j, 8), 8)] = total
            return 0

        lax.fori_loop(0, NBR, step, 0)

    energy_sum(2)

    def full(tile, _):
        dress_tile(tile, natural, result, pair_coef, atom_coef, None, middle, turned)
        return 0

    lax.fori_loop(0, TILES, full, 0)
    copies = []
    for half in range(2):
        copies.append(pltpu.make_async_copy(result.at[pl.ds(ROW * half, ROW)], out.at[energy_of(2 + half, core)], sem.at[half]))
        copies[-1].start()
    energy_sum(0)

    def part(tile, _):
        dress_tile(tile, natural, None, pair_coef, atom_coef, None, middle, turned)
        partial[tile] = turned[1]
        return 0

    lax.fori_loop(0, TILES, part, 0)
    for copy in copies:
        copy.wait()


def last_kernel(outer, partial, pair_coef, atom_coef, weights, begun, out, natural, result, middle, turned, sem):
    core = lax.axis_index("energy") % 2
    near, far = weights[0], weights[1]
    for half in range(2):
        a = outer[2 * NBR * half : 2 * NBR * half + NBR]
        b = outer[2 * NBR * half + NBR : 2 * NBR * half + 2 * NBR]
        lanes = slice(128 * half, 128 * half + 128)
        natural[0:ROW, lanes] = (near * a + far * b).reshape(ROW, LANES)
        natural[ROW : 2 * ROW, lanes] = (far * a).reshape(ROW, LANES)
    tails = outer[4 * NBR : PACK].reshape(TAIL * 8, LANES)
    near_row, far_row = near[0:1], far[0:1]
    for half in range(2):
        a = tails[:, 32 * half : 32 * half + 32]
        b = tails[:, 64 + 32 * half : 96 + 32 * half]
        natural[TAIL * 8 * half : TAIL * 8 * (half + 1), 256:288] = near_row[:, 0:32] * a + far_row[:, 0:32] * b
        natural[ROW + TAIL * 8 * half : ROW + TAIL * 8 * (half + 1), 256:288] = far_row[:, 0:32] * a

    def full(tile, _):
        dress_tile(tile, natural, result, pair_coef, atom_coef, partial, middle, turned)
        return 0

    copies = [pltpu.make_async_copy(result.at[pl.ds(ROW * half, ROW)], out.at[energy_of(half, core)], sem.at[half]) for half in range(2)]
    lax.fori_loop(0, 3, full, 0)
    copies[0].start()
    lax.fori_loop(3, TILES, full, 0)
    copies[1].start()
    for copy in copies:
        copy.wait()


def local(green_blocks, coupling, neighbours, freq_offset, emit_weight, absorb_weight):
    energies, atoms = lax.axis_size("energy"), lax.axis_size("atom")
    shape = jax.ShapeDtypeStruct
    vmem = pl.BlockSpec(memory_space=pltpu.VMEM)
    anywhere = pl.BlockSpec(memory_space=pl.ANY)
    green = jnp.transpose(green_blocks, (0, 2, 1, 3))
    outer, inner, flat = pl.pallas_call(
        pack_kernel,
        out_shape=(shape((PACK, 8, LANES), F32), shape((2, NBR, ATOM, WIDTH), F32), shape((ATOM, 2 * LANES), F32)),
        in_specs=[anywhere, vmem],
        out_specs=(vmem, vmem, vmem),
        scratch_shapes=[pltpu.VMEM((2 * NBR, ATOM, WIDTH), F32), pltpu.SemaphoreType.DMA((4,))],
        name="pack",
    )(green, jnp.transpose(coupling, (1, 0, 2)))

    pairs = []
    for e in range(energies):
        for a in range(atoms):
            if e in (0, energies - 1):
                to = e * atoms + (a ^ 1)
            else:
                to = (e + 1 if e % 2 else e - 1) * atoms + a
            pairs.append((e * atoms + a, to))
    far = lax.ppermute(outer, ("energy", "atom"), pairs)
    near = lax.ppermute(inner, "energy", [(e, e ^ 1) for e in range(energies)])
    blocks = [lax.ppermute(flat, "atom", [(a, (a - step) % atoms) for a in range(atoms)]) for step in (1, 3, 2)]
    scratch = [pltpu.VMEM((TILES * LANES, WIDTH), F32), pltpu.VMEM((TILES * LANES, WIDTH), F32), pltpu.VMEM((2 * WIDTH, LANES), F32), pltpu.VMEM((2, WIDTH, LANES), F32), pltpu.SemaphoreType.DMA((2,))]
    rows = shape((ROWS, ROW, WIDTH), F32)
    begun, partial, pair_coef, atom_coef, weights = pl.pallas_call(
        local_kernel,
        out_shape=(rows, shape((TILES, WIDTH, LANES), F32), shape((TILES, ORB * ORB, LANES), F32), shape((ORB * ORB, LANES), F32), shape((2, 8, LANES), F32)),
        in_specs=[vmem] * 10,
        out_specs=(anywhere, vmem, vmem, vmem, vmem),
        scratch_shapes=[pltpu.VMEM((LANES, 2 * LANES), F32), pltpu.VMEM((ATOM, LANES), F32)] + scratch,
        name="local",
    )(green, near, flat, blocks[0], blocks[2], blocks[1], neighbours, freq_offset[None], emit_weight[None], absorb_weight[None])
    out = pl.pallas_call(
        last_kernel,
        out_shape=rows,
        in_specs=[vmem] * 5 + [anywhere],
        out_specs=anywhere,
        scratch_shapes=scratch,
        input_output_aliases={5: 0},
        name="last",
    )(far, partial, pair_coef, atom_coef, weights, begun)
    return jnp.transpose(out.reshape(ROWS, NBR, ATOM, WIDTH), (0, 2, 1, 3))


def solution(mesh):
    placed = (
        P("energy", "atom", None, None),
        P("atom", None, None),
        P("atom", None),
        P(),
        P(),
        P(),
    )
    return jax.shard_map(
        local,
        mesh=mesh,
        in_specs=placed,
        out_specs=P("energy", "atom", None, None),
        check_vma=False,
    )
```

profile of v0, /device:TPU:231, one launch (start us, length us, event | category | flops | bytes accessed | tf_op | source)
XLA Modules:
  0.0 31.7 jit_solution(16342421187157425432)
XLA Ops:
  0.0 3.3 %pack.1 = (f32[153,8,128]{2,1,0:T(8,128)}, f32[2,34,8,288]{3,2,1,0:T(8,128)}, f32[8,256]{1,0:T(8,128)}) custom-call(f32[4,34,8,288]{3,2,1,0:T(8,128)} %bitcast.8, f32[12,8,12]{2,1,0:T(8,128)} %bitcast.10), custom_call_target="tpu_custom_call" | custom-call | tf_op jit(solution)/shard_map/pack/pallas_call | solution.py:214
  3.4 0.8 %collective-permute-start.1 = (f32[2,34,8,288]{3,2,1,0:T(8,128)}, f32[2,34,8,288]{3,2,1,0:T(8,128)S(1)}, u32[]{:S(2)}, u32[]{:S(2)}) collective-permute-start(f32[2,34,8,288]{3,2,1,0:T(8,128)} %get-tuple-element.14), channel_id=1, source_target_pairs={{0,4},{4,0},{8,12},{12,8},{16,20},{20,16},{24,28},{28,24},{32,36},... | collective-permute-start | bytes 1880072 | tf_op jit(solution)/shard_map/ppermute | solution.py:232
  4.1 1.3 %collective-permute-start = (f32[153,8,128]{2,1,0:T(8,128)}, f32[153,8,128]{2,1,0:T(8,128)S(1)}, u32[]{:S(2)}, u32[]{:S(2)}) collective-permute-start(f32[153,8,128]{2,1,0:T(8,128)} %get-tuple-element.13), channel_id=1, source_target_pairs={{0,1},{1,0},{2,3},{3,2},{4,8},{5,9},{6,10},{7,11},{8,4},{9,5},{10,... | collective-permute-start | bytes 1880072 | tf_op jit(solution)/shard_map/ppermute | solution.py:231
  5.4 0.2 collective-permute-start.4
  5.6 2.9 %collective-permute-start.3 = (f32[8,256]{1,0:T(8,128)}, f32[8,256]{1,0:T(8,128)S(1)}, u32[]{:S(2)}, u32[]{:S(2)}) collective-permute-start(f32[8,256]{1,0:T(8,128)} %get-tuple-element.15.flat), channel_id=1, source_target_pairs={{0,2},{1,3},{2,0},{3,1},{4,6},{5,7},{6,4},{7,5},{8,10},{9,11},{10,... | collective-permute-start | bytes 24584 | tf_op jit(solution)/shard_map/ppermute | solution.py:233
  8.5 1.6 %collective-permute-start.2 = (f32[8,256]{1,0:T(8,128)}, f32[8,256]{1,0:T(8,128)S(1)}, u32[]{:S(2)}, u32[]{:S(2)}) collective-permute-start(f32[8,256]{1,0:T(8,128)} %get-tuple-element.15.flat), channel_id=1, source_target_pairs={{0,3},{1,0},{2,1},{3,2},{4,7},{5,4},{6,5},{7,6},{8,11},{9,8},{10,9... | collective-permute-start | bytes 24584 | tf_op jit(solution)/shard_map/ppermute | solution.py:233
  10.1 3.0 %collective-permute-done.4.from_third = f32[8,256]{1,0:T(8,128)S(1)} collective-permute-done((f32[8,256]{1,0:T(8,128)}, f32[8,256]{1,0:T(8,128)S(1)}, u32[]{:S(2)}, u32[]{:S(2)}) %collective-permute-start.4) | collective-permute-done | bytes 8224 | tf_op jit(solution)/shard_map/ppermute | solution.py:233
  13.1 0.0 copy-start.2
  13.1 3.1 %collective-permute-done.3.from_second = f32[8,256]{1,0:T(8,128)S(1)} collective-permute-done((f32[8,256]{1,0:T(8,128)}, f32[8,256]{1,0:T(8,128)S(1)}, u32[]{:S(2)}, u32[]{:S(2)}) %collective-permute-start.3) | collective-permute-done | bytes 8224 | tf_op jit(solution)/shard_map/ppermute | solution.py:233
  16.3 0.0 copy-start.3
  16.3 0.0 collective-permute-done.2.from_next
  16.3 0.0 copy-start.4
  16.3 0.0 collective-permute-done.1.near
  16.3 0.0 copy-start
  16.3 0.0 copy-done.2
  16.3 0.6 %copy-done.3 = f32[8,256]{1,0:T(8,128)} copy-done((f32[8,256]{1,0:T(8,128)}, f32[8,256]{1,0:T(8,128)S(1)}, u32[]{:S(2)}) %copy-start.3) | copy-done | bytes 8216
  16.9 0.0 copy-done.4
  16.9 0.3 %copy-done = f32[2,34,8,288]{3,2,1,0:T(8,128)} copy-done((f32[2,34,8,288]{3,2,1,0:T(8,128)}, f32[2,34,8,288]{3,2,1,0:T(8,128)S(1)}, u32[]{:S(2)}) %copy-start) | copy-done | bytes 626712
  17.2 8.8 %local.1 = (f32[4,272,288]{2,1,0:T(8,128)}, f32[5,288,128]{2,1,0:T(8,128)}, f32[5,144,128]{2,1,0:T(8,128)}, f32[144,128]{1,0:T(8,128)}, f32[2,8,128]{2,1,0:T(8,128)}) custom-call(f32[4,34,8,288]{3,2,1,0:T(8,128)} %bitcast.9, f32[2,34,8,288]{3,2,1,0:T(8,128)} %copy-done, f32[8,256]{1,0:T(8,128)} %get-tuple-element.15.flat, f32[8,256]{1,0:T(8,128)} %copy-done.4, ...), custom_call_target="tpu_custom_call" | custom-call | tf_op jit(solution)/shard_map/local/pallas_call | solution.py:236
  26.0 0.0 collective-permute-done.outer
  26.0 0.0 copy-start.1
  26.0 0.8 %copy-done.1 = f32[153,8,128]{2,1,0:T(8,128)} copy-done((f32[153,8,128]{2,1,0:T(8,128)}, f32[153,8,128]{2,1,0:T(8,128)S(1)}, u32[]{:S(2)}) %copy-start.1) | copy-done | bytes 626712
  26.8 4.9 %last.1 = f32[4,272,288]{2,1,0:T(8,128)} custom-call(f32[153,8,128]{2,1,0:T(8,128)} %copy-done.1, f32[5,288,128]{2,1,0:T(8,128)} %get-tuple-element.16.partial, f32[5,144,128]{2,1,0:T(8,128)} %get-tuple-element.17.pair_coef, f32[144,128]{1,0:T(8,128)} %get-tuple-element.18.atom_coef, ...), custom_call_target="tpu_custom_call", output_to_operand_aliasing={{}: (5, {})} | custom-call | tf_op jit(solution)/shard_map/last/pallas_call | solution.py:244
Async XLA Ops:
  3.4 12.9 %collective-permute-start.1 = (f32[2,34,8,288]{3,2,1,0:T(8,128)}, f32[2,34,8,288]{3,2,1,0:T(8,128)S(1)}, u32[]{:S(2)}, u32[]{:S(2)}) collective-permute-start(f32[2,34,8,288]{3,2,1,0:T(8,128)} %get-tuple-element.14), channel_id=1, source_target_pairs={{0,4},{4,0},{8,12},{12,8},{16,20},{20,16},{24,28},{28,24},{32,36},... | collective-permute-start | bytes 1880072 | tf_op jit(solution)/shard_map/ppermute | solution.py:232
  4.1 21.8 %collective-permute-start = (f32[153,8,128]{2,1,0:T(8,128)}, f32[153,8,128]{2,1,0:T(8,128)S(1)}, u32[]{:S(2)}, u32[]{:S(2)}) collective-permute-start(f32[153,8,128]{2,1,0:T(8,128)} %get-tuple-element.13), channel_id=1, source_target_pairs={{0,1},{1,0},{2,3},{3,2},{4,8},{5,9},{6,10},{7,11},{8,4},{9,5},{10,... | collective-permute-start | bytes 1880072 | tf_op jit(solution)/shard_map/ppermute | solution.py:231
  5.4 7.7 %collective-permute-start.4 = (f32[8,256]{1,0:T(8,128)}, f32[8,256]{1,0:T(8,128)S(1)}, u32[]{:S(2)}, u32[]{:S(2)}) collective-permute-start(f32[8,256]{1,0:T(8,128)} %get-tuple-element.15.flat), channel_id=1, source_target_pairs={{0,1},{1,2},{2,3},{3,0},{4,5},{5,6},{6,7},{7,4},{8,9},{9,10},{10,1... | collective-permute-start | bytes 24584 | tf_op jit(solution)/shard_map/ppermute | solution.py:233
  5.6 10.7 %collective-permute-start.3 = (f32[8,256]{1,0:T(8,128)}, f32[8,256]{1,0:T(8,128)S(1)}, u32[]{:S(2)}, u32[]{:S(2)}) collective-permute-start(f32[8,256]{1,0:T(8,128)} %get-tuple-element.15.flat), channel_id=1, source_target_pairs={{0,2},{1,3},{2,0},{3,1},{4,6},{5,7},{6,4},{7,5},{8,10},{9,11},{10,... | collective-permute-start | bytes 24584 | tf_op jit(solution)/shard_map/ppermute | solution.py:233
  8.5 7.8 %collective-permute-start.2 = (f32[8,256]{1,0:T(8,128)}, f32[8,256]{1,0:T(8,128)S(1)}, u32[]{:S(2)}, u32[]{:S(2)}) collective-permute-start(f32[8,256]{1,0:T(8,128)} %get-tuple-element.15.flat), channel_id=1, source_target_pairs={{0,3},{1,0},{2,1},{3,2},{4,7},{5,4},{6,5},{7,6},{8,11},{9,8},{10,9... | collective-permute-start | bytes 24584 | tf_op jit(solution)/shard_map/ppermute | solution.py:233
  13.1 3.2 %copy-start.2 = (f32[8,256]{1,0:T(8,128)}, f32[8,256]{1,0:T(8,128)S(1)}, u32[]{:S(2)}) copy-start(f32[8,256]{1,0:T(8,128)S(1)} %collective-permute-done.4.from_third) | copy-start | bytes 24580
  16.3 0.6 %copy-start.3 = (f32[8,256]{1,0:T(8,128)}, f32[8,256]{1,0:T(8,128)S(1)}, u32[]{:S(2)}) copy-start(f32[8,256]{1,0:T(8,128)S(1)} %collective-permute-done.3.from_second) | copy-start | bytes 24580
  16.3 0.6 %copy-start.4 = (f32[8,256]{1,0:T(8,128)}, f32[8,256]{1,0:T(8,128)S(1)}, u32[]{:S(2)}) copy-start(f32[8,256]{1,0:T(8,128)S(1)} %collective-permute-done.2.from_next) | copy-start | bytes 24580
  16.3 0.9 %copy-start = (f32[2,34,8,288]{3,2,1,0:T(8,128)}, f32[2,34,8,288]{3,2,1,0:T(8,128)S(1)}, u32[]{:S(2)}) copy-start(f32[2,34,8,288]{3,2,1,0:T(8,128)S(1)} %collective-permute-done.1.near) | copy-start | bytes 1880068
  26.0 0.8 %copy-start.1 = (f32[153,8,128]{2,1,0:T(8,128)}, f32[153,8,128]{2,1,0:T(8,128)S(1)}, u32[]{:S(2)}) copy-start(f32[153,8,128]{2,1,0:T(8,128)S(1)} %collective-permute-done.outer) | copy-start | bytes 1880068
where the time goes:
time: 31.9 us; the launch traced here: 31.7 us
  Pallas kernels  17 us (53%)
  starting transfers between devices  6.75 us (21%)
  waiting for transfers between devices  6.16 us (19%)
  local copies, waits for them, and re-layouts  1.73 us (5%)
    pallas_call x1, Pallas kernels, local(): pl.pallas_call(local_kernel, out_shape=(rows, shape((TILES, WIDTH, LANES)...  8.75 us
    ppermute x3, waiting for transfers between devices, local(): lax.ppermute(flat, 'atom', [(a, (a - step) % atoms) for a in range(atoms)])  6.15 us
    pallas_call x1, Pallas kernels, local(): pl.pallas_call(last_kernel, out_shape=rows, in_specs=[vmem] * 5 + [anywhe...  4.86 us
    ppermute x3, starting transfers between devices, local(): lax.ppermute(flat, 'atom', [(a, (a - step) % atoms) for a in range(atoms)])  4.69 us
    pallas_call x1, Pallas kernels, local(): pl.pallas_call(pack_kernel, out_shape=(shape((PACK, 8, LANES), F32), shap...  3.35 us
    unnamed x10, local copies, waits for them, and re-layouts  1.73 us
    ppermute x1, starting transfers between devices, local(): far = lax.ppermute(outer, ('energy', 'atom'), pairs)  1.3 us
    ppermute x1, starting transfers between devices, local(): near = lax.ppermute(inner, 'energy', [(e, e ^ 1) for e in range(energies)])  0.76 us
  transfers between devices with their start and end apart: 5, of which 2 were waited for; matrix products, arithmetic and copies ran while one was open for 0% of the time, Pallas kernels for 28%

commit v1 on v0

v1 whole, which is shorter than its diff:
```python
import jax
import jax.numpy as jnp
from jax import lax
from jax.experimental import pallas as pl
from jax.experimental.pallas import tpu as pltpu
from jax.sharding import PartitionSpec as P

OFF = 2
ROWS = 4
ORB = 12
NBR = 34
ATOM = 8
ROW = NBR * ATOM
WIDTH = 288
LANES = 128
TILES = 5
TAIL = 17
PACK = 4 * NBR + TAIL
F32 = jnp.float32
BF16 = jnp.bfloat16
GRANT = 16 << 20


def energy_of(row, core):
    return jnp.where(core == 0, row, ROWS - 1 - row)


def pack_kernel(green, outer, fore, rear, sem):
    core = lax.axis_index("energy") % 2
    copies = []
    for row in range(ROWS):
        target = fore.at[row] if row < 2 else rear.at[row - 2]
        copies.append(pltpu.make_async_copy(green.at[energy_of(row, core)], target, sem.at[row]))
    for copy in copies:
        copy.start()
    for row in range(2):
        copies[row].wait()
        outer[NBR * row : NBR * (row + 1)] = fore[row, :, :, 0:128]
        outer[NBR * (2 + row) : NBR * (3 + row)] = fore[row, :, :, 128:256]
    tails = [fore[part // 2, TAIL * (part % 2) : TAIL * (part % 2 + 1), :, 256:288] for part in range(4)]
    outer[4 * NBR : PACK] = jnp.concatenate(tails, axis=-1)
    copies[2].wait()
    copies[3].wait()


def turn_in(tile, natural, x):
    rows = slice(LANES * tile, LANES * (tile + 1))
    x[tile, 0:128] = natural[rows, 0:128].T
    x[tile, 128:256] = natural[rows, 128:256].T
    x[tile, 256:288] = natural[rows, 256:288].T


def turn_out(tile, result, y):
    rows = slice(LANES * tile, LANES * (tile + 1))
    result[rows, 0:128] = y[tile, 0:128].T
    result[rows, 128:256] = y[tile, 128:256].T
    result[rows, 256:288] = y[tile, 256:288].T


def left(tile, atom_coef, x, z):
    low = lax.broadcasted_iota(jnp.int32, (8, LANES), 0) < 4
    for a in range(ORB):
        totals = [[None] * 3 for _ in range(2)]
        for pair in range(6):
            first = jnp.broadcast_to(atom_coef[ORB * a + 2 * pair : ORB * a + 2 * pair + 1], (8, LANES))
            last = jnp.broadcast_to(atom_coef[ORB * a + 2 * pair + 1 : ORB * a + 2 * pair + 2], (8, LANES))
            coef = (first, jnp.where(low, first, last), last)
            for part in range(2):
                for k in range(3):
                    term = coef[k] * x[tile, pl.ds(144 * part + 24 * pair + 8 * k, 8)]
                    totals[part][k] = term if pair == 0 else totals[part][k] + term
        for part in range(2):
            for k in range(3):
                z[tile, pl.ds((ORB * part + a) * 24 + 8 * k, 8)] = totals[part][k]


def right(tile, pair_coef, z, y):
    values = []
    for d in range(ORB):
        values.append([z[tile, pl.ds(192 * k + d, 8, stride=24)] + z[tile, pl.ds(192 * k + 12 + d, 8, stride=24)] for k in range(3)])
    for f in range(ORB):
        totals = [None] * 3
        for d in range(ORB):
            coef = jnp.broadcast_to(pair_coef[tile, ORB * f + d : ORB * f + d + 1], (8, LANES))
            for k in range(3):
                term = coef * values[d][k]
                totals[k] = term if d == 0 else totals[k] + term
        for k in range(3):
            y[tile, pl.ds(96 * k + f, 8, stride=ORB)] = totals[k]


def coupling_rows(block):
    rows = jnp.concatenate([block[orbital] for orbital in range(ORB)] + [jnp.zeros((ATOM, 2 * LANES - ORB * ORB), F32)], axis=-1)
    high = rows.astype(BF16).astype(F32)
    mid = (rows - high).astype(BF16).astype(F32)
    return high, mid, rows - high - mid


def kernel_values(freq, emit, absorb, sign):
    sums = []
    for d in range(-OFF, OFF + 1):
        shift = d * sign
        terms = jnp.where(freq == -shift, emit, 0.0) + jnp.where(freq == shift, absorb, 0.0)
        sums.append(jnp.sum(terms, axis=1, keepdims=True))
    return sums


def sum_kernel(fore, rear, neighbours, freq, emit, absorb, sums, weights, chosen, indices):
    position = lax.axis_index("energy")
    core = position % 2
    weight = kernel_values(freq[...], emit[...], absorb[...], 1 - 2 * core)
    inside = jnp.where((position > 0) & (position < lax.axis_size("energy") - 1), 1.0, 0.0).astype(F32)
    for place, value in enumerate((weight[1] * inside, weight[0] * inside, weight[3], weight[4])):
        weights[place] = jnp.broadcast_to(value, (8, LANES))
    indices[...] = jnp.zeros_like(indices)
    indices[:, 0:NBR] = neighbours[...].astype(F32)
    width = TILES * LANES
    lane = lax.broadcasted_iota(jnp.int32, (LANES, width), 1)
    within = lane - jnp.where(lane >= ROW, ROW, 0) - jnp.where(lane >= 2 * ROW, ROW, 0)
    picks = (lax.shift_right_logical(within, 3) == lax.broadcasted_iota(jnp.int32, (LANES, width), 0)).astype(F32).astype(BF16)
    spread = jnp.dot(indices[...].astype(BF16), picks, preferred_element_type=F32)
    lane8 = lax.broadcasted_iota(jnp.int32, (ATOM, width), 1) & 7
    own = lane8 == lax.broadcasted_iota(jnp.int32, (ATOM, width), 0)
    listed = jnp.sum(jnp.where(own, spread, 0.0), axis=0, keepdims=True)
    listed = listed - (lax.axis_index("atom") * ATOM).astype(F32)
    listed = jnp.where(listed < 0, listed + 32.0, listed)
    number = (lax.broadcasted_iota(jnp.int32, (LANES, width), 0) & 31).astype(F32)
    chosen[:, 0:width] = (number == listed).astype(F32).astype(BF16)
    spots = (lax.broadcasted_iota(jnp.int32, (LANES, LANES), 0) & 31) == (lax.broadcasted_iota(jnp.int32, (LANES, LANES), 1) & 7)
    chosen[:, width : width + LANES] = spots.astype(F32).astype(BF16)

    def step(j, _):
        for sub in range(2):
            values = [fore[0, 2 * j + sub], fore[1, 2 * j + sub], rear[0, 2 * j + sub], rear[1, 2 * j + sub]]
            for row in range(ROWS):
                total = None
                for source in range(ROWS):
                    if abs(source - row) <= OFF:
                        term = weight[source - row + OFF] * values[source]
                        total = term if total is None else total + term
                sums[row, 2 * j + sub] = total
        return 0

    lax.fori_loop(0, NBR // 2, step, 0)


def left_kernel(sums, weights, near, mine, chosen, atom_coef, z, every, natural, x):
    every[...] = jnp.zeros_like(every)
    for place, part in enumerate(coupling_rows(mine)):
        every[32 * place : 32 * place + 8] = part
    columns = every[...].T[0 : ORB * ORB].astype(BF16)
    atom_coef[...] = jnp.dot(columns, chosen[:, LANES * TILES : LANES * (TILES + 1)], preferred_element_type=F32)
    first, second = weights[2][0:1, 0:1], weights[3][0:1, 0:1]

    def step(j, _):
        for sub in range(2):
            place = 2 * j + sub
            a, b = near[1, place], near[0, place]
            natural[pl.ds(pl.multiple_of(8 * place, 8), 8)] = sums[2, place] + second * a
            natural[pl.ds(pl.multiple_of(ROW + 8 * place, 8), 8)] = sums[3, place] + (first * a + second * b)
        return 0

    lax.fori_loop(0, NBR // 2, step, 0)
    turn_in(0, natural, x)
    for tile in range(TILES):
        if tile + 1 < TILES:
            turn_in(tile + 1, natural, x)
        left(tile, atom_coef, x, z)


def sender(result, out, first_row, core, sem):
    copies = [pltpu.make_async_copy(result.at[pl.ds(ROW * half, ROW)], out.at[energy_of(first_row + half, core)], sem.at[half]) for half in range(2)]

    def after(tile):
        if tile == 2:
            copies[0].start()
        if tile == TILES - 1:
            copies[1].start()

    return copies, after


def right_kernel(z, chosen, mine, from_next, from_second, from_third, out, pair_coef, every, result, y, sem):
    position = lax.axis_index("energy")
    crossed = jnp.where((position == 1) | (position == lax.axis_size("energy") - 2), 1, 0)
    for place, block in ((0, mine), (1 + 2 * crossed, from_next), (2, from_second), (3 - 2 * crossed, from_third)):
        for part, rows in enumerate(coupling_rows(block)):
            every[pl.ds(pl.multiple_of(32 * part + 8 * place, 8), 8)] = rows
    every[96:128] = jnp.zeros((32, 2 * LANES), F32)
    columns = every[...].T[0 : ORB * ORB].astype(BF16)
    for tile in range(TILES):
        pair_coef[tile] = jnp.dot(columns, chosen[:, LANES * tile : LANES * (tile + 1)], preferred_element_type=F32)
    copies, after = sender(result, out, 2, lax.axis_index("energy") % 2, sem)
    for tile in range(TILES):
        right(tile, pair_coef, z, y)
        turn_out(tile, result, y)
        after(tile)
    for copy in copies:
        copy.wait()


def last_kernel(outer, sums, pair_coef, atom_coef, weights, begun, out, natural, result, x, z, y, sem):
    near, far = weights[0], weights[1]
    for half in range(2):
        a = outer[2 * NBR * half : 2 * NBR * half + NBR]
        b = outer[2 * NBR * half + NBR : 2 * NBR * half + 2 * NBR]
        lanes = slice(128 * half, 128 * half + 128)
        natural[0:ROW, lanes] = (sums[0, :, :, lanes] + (near * a + far * b)).reshape(ROW, LANES)
        natural[ROW : 2 * ROW, lanes] = (sums[1, :, :, lanes] + far * a).reshape(ROW, LANES)
    near_part, far_part = near[0:1, 0:32], far[0:1, 0:32]
    for half in range(2):
        a = outer[4 * NBR : PACK, :, 32 * half : 32 * half + 32]
        b = outer[4 * NBR : PACK, :, 64 + 32 * half : 96 + 32 * half]
        rows = slice(TAIL * 8 * half, TAIL * 8 * (half + 1))
        tiles = slice(TAIL * half, TAIL * (half + 1))
        natural[rows, 256:288] = (sums[0, tiles, :, 256:288] + (near_part * a + far_part * b)).reshape(TAIL * 8, 32)
        rows = slice(ROW + TAIL * 8 * half, ROW + TAIL * 8 * (half + 1))
        natural[rows, 256:288] = (sums[1, tiles, :, 256:288] + far_part * a).reshape(TAIL * 8, 32)
    copies, after = sender(result, out, 0, lax.axis_index("energy") % 2, sem)
    turn_in(0, natural, x)
    for tile in range(TILES):
        if tile + 1 < TILES:
            turn_in(tile + 1, natural, x)
        left(tile, atom_coef, x, z)
        right(tile, pair_coef, z, y)
        turn_out(tile, result, y)
        after(tile)
    for copy in copies:
        copy.wait()


def held(value):
    return pltpu.with_memory_space_constraint(value, pltpu.VMEM)


def planned(green_blocks, coupling, neighbours, freq_offset, emit_weight, absorb_weight):
    energies, atoms = lax.axis_size("energy"), lax.axis_size("atom")
    shape = lambda dims, dtype=F32: pltpu.VMEM(dims, dtype)
    vmem = pl.BlockSpec(memory_space=pltpu.VMEM)
    anywhere = pl.BlockSpec(memory_space=pl.ANY)
    green = jnp.transpose(green_blocks, (0, 2, 1, 3))
    mine = jnp.transpose(coupling, (1, 0, 2))
    ends = {0: 1, energies - 1: energies - 2}
    others = {other: end for end, other in ends.items()}
    up, down = [], []
    for e in range(energies):
        for a in range(atoms):
            here, above, below = e * atoms + a, (a + 1) % atoms, (a - 1) % atoms
            if e in ends:
                up.append((here, ends[e] * atoms + below))
                down.append((here, e * atoms + below))
            elif e in others:
                up.append((here, others[e] * atoms + above))
                down.append((here, e * atoms + above))
            else:
                up.append((here, e * atoms + above))
                down.append((here, e * atoms + below))
    third = lax.ppermute(mine, ("energy", "atom"), up)
    first = lax.ppermute(mine, ("energy", "atom"), down)
    outer, fore, rear = pl.pallas_call(
        pack_kernel,
        out_shape=(shape((PACK, 8, LANES)), shape((2, NBR, ATOM, WIDTH)), shape((2, NBR, ATOM, WIDTH))),
        in_specs=[pl.BlockSpec(memory_space=pltpu.HBM)],
        out_specs=(vmem, vmem, vmem),
        scratch_shapes=[pltpu.SemaphoreType.DMA((ROWS,))],
        compiler_params=pltpu.CompilerParams(vmem_limit_bytes=GRANT),
        name="pack",
    )(pltpu.with_memory_space_constraint(green, pltpu.HBM))

    pairs = []
    for e in range(energies):
        for a in range(atoms):
            if e in (0, energies - 1):
                to = e * atoms + (a + 1) % atoms
            else:
                to = (e + 1 if e % 2 else e - 1) * atoms + a
            pairs.append((e * atoms + a, to))
    far = lax.ppermute(outer, ("energy", "atom"), pairs)
    near = lax.ppermute(rear, "energy", [(e, e ^ 1) for e in range(energies)])
    second = lax.ppermute(mine, "atom", [(a, (a + 2) % atoms) for a in range(atoms)])
    sums, weights, chosen = pl.pallas_call(
        sum_kernel,
        out_shape=(shape((ROWS, NBR, ATOM, WIDTH)), shape((4, 8, LANES)), shape((LANES, (TILES + 1) * LANES), BF16)),
        in_specs=[vmem] * 6,
        out_specs=(vmem, vmem, vmem),
        scratch_shapes=[pltpu.VMEM((ATOM, LANES), F32)],
        compiler_params=pltpu.CompilerParams(vmem_limit_bytes=GRANT),
        name="sums",
    )(fore, rear, neighbours, freq_offset[None], emit_weight[None], absorb_weight[None])
    turned = pltpu.VMEM((TILES, WIDTH, LANES), F32)
    halfway = shape((TILES, 2 * WIDTH, LANES))
    rowwise = pltpu.VMEM((TILES * LANES, WIDTH), F32)
    table = pltpu.VMEM((LANES, 2 * LANES), F32)
    rows = jax.ShapeDtypeStruct((ROWS, ROW, WIDTH), F32)
    atom_coef, z = pl.pallas_call(
        left_kernel,
        out_shape=(shape((ORB * ORB, LANES)), halfway),
        in_specs=[vmem] * 5,
        out_specs=(vmem, vmem),
        scratch_shapes=[table, rowwise, turned],
        compiler_params=pltpu.CompilerParams(vmem_limit_bytes=GRANT),
        name="left",
    )(*map(held, (sums, weights, near, mine, chosen)))
    begun, pair_coef = pl.pallas_call(
        right_kernel,
        out_shape=(rows, shape((TILES, ORB * ORB, LANES))),
        in_specs=[vmem] * 6,
        out_specs=(anywhere, vmem),
        scratch_shapes=[table, rowwise, turned, pltpu.SemaphoreType.DMA((2,))],
        compiler_params=pltpu.CompilerParams(vmem_limit_bytes=GRANT),
        name="right",
    )(*map(held, (z, chosen, mine, first, second, third)))
    out = pl.pallas_call(
        last_kernel,
        out_shape=rows,
        in_specs=[vmem] * 5 + [anywhere],
        out_specs=anywhere,
        scratch_shapes=[rowwise, rowwise, turned, halfway, turned, pltpu.SemaphoreType.DMA((2,))],
        input_output_aliases={5: 0},
        compiler_params=pltpu.CompilerParams(vmem_limit_bytes=GRANT),
        name="last",
    )(*map(held, (far, sums, pair_coef, atom_coef, weights)), begun)
    return jnp.transpose(out.reshape(ROWS, NBR, ATOM, WIDTH), (0, 2, 1, 3))


def solution(mesh):
    placed = (
        P("energy", "atom", None, None),
        P("atom", None, None),
        P("atom", None),
        P(),
        P(),
        P(),
    )
    return jax.shard_map(
        planned,
        mesh=mesh,
        in_specs=placed,
        out_specs=P("energy", "atom", None, None),
        check_vma=False,
    )
```

time: 31.9 us -> 21 us (0.66)
  Pallas kernels: 17 us -> 8.86 us
  local copies, waits for them, and re-layouts: 1.73 us -> 0.02 us
  starting transfers between devices: 6.75 us -> 5.75 us
    pallas_call x3 -> x5, Pallas kernels: 17 us -> 8.86 us  [the longest x1 2.77 us: planned(): pl.pallas_call(last_kernel, out_shape=rows, in_specs=[vmem] * 5 + [anywhe...]
    unnamed x10, local copies, waits for them, and re-layouts: 1.73 us -> 0.02 us
    ppermute x5, starting transfers between devices: 6.75 us -> 5.75 us  [the longest x1 2.27 us: planned(): third = lax.ppermute(mine, ('energy', 'atom'), up)]
  transfers between devices with their start and end apart: 5 -> 5, of which waited for: 2 -> 1; matrix products, arithmetic and copies ran while one was open for 0% -> 0% of each run, Pallas kernels for 28% -> 22%
where the time goes in v1:
time: 21 us; the launch traced here: 20.9 us
  Pallas kernels  8.86 us (42%)
  waiting for transfers between devices  6.21 us (30%)
  starting transfers between devices  5.75 us (27%)
    ppermute x1, waiting for transfers between devices, planned(): lax.ppermute(mine, 'atom', [(a, (a + 2) % atoms) for a in range(atoms)])  6.2 us
    pallas_call x1, Pallas kernels, planned(): pl.pallas_call(last_kernel, out_shape=rows, in_specs=[vmem] * 5 + [anywhe...  2.77 us
    ppermute x1, starting transfers between devices, planned(): third = lax.ppermute(mine, ('energy', 'atom'), up)  2.27 us
    pallas_call x1, Pallas kernels, planned(): pl.pallas_call(right_kernel, out_shape=(rows, shape((TILES, ORB * ORB, LA...  2.17 us
    pallas_call x1, Pallas kernels, planned(): pl.pallas_call(left_kernel, out_shape=(shape((ORB * ORB, LANES)), halfway...  1.86 us
    pallas_call x1, Pallas kernels, planned(): pl.pallas_call(pack_kernel, out_shape=(shape((PACK, 8, LANES)), shape((2,...  1.47 us
    ppermute x1, starting transfers between devices, planned(): far = lax.ppermute(outer, ('energy', 'atom'), pairs)  1.3 us
    ppermute x1, starting transfers between devices, planned(): first = lax.ppermute(mine, ('energy', 'atom'), down)  1.07 us
  transfers between devices with their start and end apart: 5, of which 1 were waited for; matrix products, arithmetic and copies ran while one was open for 0% of the time, Pallas kernels for 22%

profile of v1, /device:TPU:231, one launch (start us, length us, event | category | flops | bytes accessed | tf_op | source)
XLA Modules:
  0.0 20.9 jit_solution(2486312117110300201)
XLA Ops:
  0.0 0.0 copy-start
  0.0 0.0 copy-start.4
  0.0 0.0 copy-start.3
  0.0 0.0 copy-start.2
  0.0 0.0 copy-start.1
  0.0 1.5 %pack.1 = (f32[153,8,128]{2,1,0:T(8,128)S(1)}, f32[2,34,8,288]{3,2,1,0:T(8,128)S(1)}, f32[2,34,8,288]{3,2,1,0:T(8,128)S(1)}) custom-call(f32[4,34,8,288]{3,2,1,0:T(8,128)} %bitcast.16), custom_call_target="tpu_custom_call" | custom-call | tf_op jit(solution)/shard_map/pack/pallas_call | solution.py:260
  1.5 0.8 %collective-permute-start.1 = (f32[2,34,8,288]{3,2,1,0:T(8,128)S(1)}, f32[2,34,8,288]{3,2,1,0:T(8,128)S(1)}, u32[]{:S(2)}, u32[]{:S(2)}) collective-permute-start(f32[2,34,8,288]{3,2,1,0:T(8,128)S(1)} %get-tuple-element.17.rear), channel_id=1, source_target_pairs={{0,4},{4,0},{8,12},{12,8},{16,20},{20,16},{24,28},{28,24},{32,36},... | collective-permute-start | bytes 1880072 | tf_op jit(solution)/shard_map/ppermute | solution.py:279
  2.3 1.3 %collective-permute-start = (f32[153,8,128]{2,1,0:T(8,128)S(1)}, f32[153,8,128]{2,1,0:T(8,128)S(1)}, u32[]{:S(2)}, u32[]{:S(2)}) collective-permute-start(f32[153,8,128]{2,1,0:T(8,128)S(1)} %get-tuple-element.15), channel_id=1, source_target_pairs={{0,1},{1,2},{2,3},{3,0},{4,8},{5,9},{6,10},{7,11},{8,4},{9,5},{10,... | collective-permute-start | bytes 1880072 | tf_op jit(solution)/shard_map/ppermute | solution.py:278
  3.6 0.0 copy-done
  3.6 2.3 %collective-permute-start.4 = (f32[12,8,12]{2,1,0:T(8,128)S(1)}, f32[12,8,12]{2,1,0:T(8,128)S(1)}, u32[]{:S(2)}, u32[]{:S(2)}) collective-permute-start(f32[12,8,12]{2,1,0:T(8,128)S(1)} %bitcast.8), channel_id=1, source_target_pairs={{0,7},{1,4},{2,5},{3,6},{4,1},{5,2},{6,3},{7,0},{8,9},{9,10},{10,1... | collective-permute-start | bytes 13832 | tf_op jit(solution)/shard_map/ppermute | solution.py:258
  5.8 0.4 %collective-permute-start.3 = (f32[12,8,12]{2,1,0:T(8,128)S(1)}, f32[12,8,12]{2,1,0:T(8,128)S(1)}, u32[]{:S(2)}, u32[]{:S(2)}) collective-permute-start(f32[12,8,12]{2,1,0:T(8,128)S(1)} %bitcast.9), channel_id=1, source_target_pairs={{0,2},{1,3},{2,0},{3,1},{4,6},{5,7},{6,4},{7,5},{8,10},{9,11},{10,... | collective-permute-start | bytes 13832 | tf_op jit(solution)/shard_map/ppermute | solution.py:280
  6.2 1.1 %collective-permute-start.2 = (f32[12,8,12]{2,1,0:T(8,128)S(1)}, f32[12,8,12]{2,1,0:T(8,128)S(1)}, u32[]{:S(2)}, u32[]{:S(2)}) collective-permute-start(f32[12,8,12]{2,1,0:T(8,128)S(1)} %bitcast.10), channel_id=1, source_target_pairs={{0,3},{1,0},{2,1},{3,2},{4,5},{5,6},{6,7},{7,4},{8,11},{9,8},{10,9... | collective-permute-start | bytes 13832 | tf_op jit(solution)/shard_map/ppermute | solution.py:259
  7.3 0.0 copy-done.4
  7.3 0.0 copy-done.3
  7.3 0.0 copy-done.2
  7.3 0.0 copy-done.1
  7.3 0.6 %sums.1 = (f32[4,34,8,288]{3,2,1,0:T(8,128)S(1)}, f32[4,8,128]{2,1,0:T(8,128)S(1)}, bf16[128,768]{1,0:T(8,128)(2,1)S(1)}) custom-call(f32[2,34,8,288]{3,2,1,0:T(8,128)S(1)} %get-tuple-element.16.fore, f32[2,34,8,288]{3,2,1,0:T(8,128)S(1)} %get-tuple-element.17.rear, s32[8,34]{1,0:T(8,128)S(1)} %copy-done.1, s32[1,64]{1,0:T(1,128)S(1)} %bitcast.13, ...), custom_call_target="tpu_custom_call" | custom-call | tf_op jit(solution)/shard_map/sums/pallas_call | solution.py:281
  7.9 0.0 collective-permute-done.1.near
  7.9 1.9 %left.1 = (f32[144,128]{1,0:T(8,128)S(1)}, f32[5,576,128]{2,1,0:T(8,128)S(1)}) custom-call(f32[4,34,8,288]{3,2,1,0:T(8,128)S(1)} %get-tuple-element.18.sums, f32[4,8,128]{2,1,0:T(8,128)S(1)} %get-tuple-element.19.weights, f32[2,34,8,288]{3,2,1,0:T(8,128)S(1)} %collective-permute-done.1.near, f32[12,8,12]{2,1,0:T(8,128)S(1)} %bitcast.11, ...), custom_call_target="tpu_custom_call" | custom-call | tf_op jit(solution)/shard_map/left/pallas_call | solution.py:295
  9.7 0.0 collective-permute-done.4.from_third
  9.8 6.2 %collective-permute-done.3.from_second = f32[12,8,12]{2,1,0:T(8,128)S(1)} collective-permute-done((f32[12,8,12]{2,1,0:T(8,128)S(1)}, f32[12,8,12]{2,1,0:T(8,128)S(1)}, u32[]{:S(2)}, u32[]{:S(2)}) %collective-permute-start.3) | collective-permute-done | bytes 4640 | tf_op jit(solution)/shard_map/ppermute | solution.py:280
  16.0 0.0 collective-permute-done.2.from_next
  16.0 2.2 %right.1 = (f32[4,272,288]{2,1,0:T(8,128)}, f32[5,144,128]{2,1,0:T(8,128)S(1)}) custom-call(f32[5,576,128]{2,1,0:T(8,128)S(1)} %get-tuple-element.21.z, bf16[128,768]{1,0:T(8,128)(2,1)S(1)} %get-tuple-element.20.chosen, f32[12,8,12]{2,1,0:T(8,128)S(1)} %bitcast.12, f32[12,8,12]{2,1,0:T(8,128)S(1)} %collective-permute-done.2.from_next, ...), custom_call_target="tpu_custom_call" | custom-call | tf_op jit(solution)/shard_map/right/pallas_call | solution.py:304
  18.1 0.0 collective-permute-done.outer
  18.1 2.8 %last.1 = f32[4,272,288]{2,1,0:T(8,128)} custom-call(f32[153,8,128]{2,1,0:T(8,128)S(1)} %collective-permute-done.outer, f32[4,34,8,288]{3,2,1,0:T(8,128)S(1)} %get-tuple-element.18.sums, f32[5,144,128]{2,1,0:T(8,128)S(1)} %get-tuple-element.22.pair_coef, f32[144,128]{1,0:T(8,128)S(1)} %get-tuple-element.23.atom_coef, ...), custom_call_target="tpu_custom_call", output_to_operand_aliasing={{}: (5, {})} | custom-call | tf_op jit(solution)/shard_map/last/pallas_call | solution.py:313
Async XLA Ops:
  0.0 3.6 %copy-start = (f32[8,12,12]{2,0,1:T(8,128)S(1)}, f32[8,12,12]{2,0,1:T(8,128)}, u32[]{:S(2)}) copy-start(f32[8,12,12]{2,0,1:T(8,128)} %param.7) | copy-start | bytes 13828
  0.0 7.3 %copy-start.4 = (f32[64]{0:T(128)S(1)}, f32[64]{0:T(128)}, u32[]{:S(2)}) copy-start(f32[64]{0:T(128)} %param.11) | copy-start | bytes 772
  0.0 7.3 %copy-start.3 = (f32[64]{0:T(128)S(1)}, f32[64]{0:T(128)}, u32[]{:S(2)}) copy-start(f32[64]{0:T(128)} %param.10) | copy-start | bytes 772
  0.0 7.3 %copy-start.2 = (s32[64]{0:T(128)S(1)}, s32[64]{0:T(128)}, u32[]{:S(2)}) copy-start(s32[64]{0:T(128)} %param.9) | copy-start | bytes 772
  0.0 7.3 %copy-start.1 = (s32[8,34]{1,0:T(8,128)S(1)}, s32[8,34]{1,0:T(8,128)}, u32[]{:S(2)}) copy-start(s32[8,34]{1,0:T(8,128)} %neighbours.1) | copy-start | bytes 3268
  1.5 6.4 %collective-permute-start.1 = (f32[2,34,8,288]{3,2,1,0:T(8,128)S(1)}, f32[2,34,8,288]{3,2,1,0:T(8,128)S(1)}, u32[]{:S(2)}, u32[]{:S(2)}) collective-permute-start(f32[2,34,8,288]{3,2,1,0:T(8,128)S(1)} %get-tuple-element.17.rear), channel_id=1, source_target_pairs={{0,4},{4,0},{8,12},{12,8},{16,20},{20,16},{24,28},{28,24},{32,36},... | collective-permute-start | bytes 1880072 | tf_op jit(solution)/shard_map/ppermute | solution.py:279
  2.3 15.9 %collective-permute-start = (f32[153,8,128]{2,1,0:T(8,128)S(1)}, f32[153,8,128]{2,1,0:T(8,128)S(1)}, u32[]{:S(2)}, u32[]{:S(2)}) collective-permute-start(f32[153,8,128]{2,1,0:T(8,128)S(1)} %get-tuple-element.15), channel_id=1, source_target_pairs={{0,1},{1,2},{2,3},{3,0},{4,8},{5,9},{6,10},{7,11},{8,4},{9,5},{10,... | collective-permute-start | bytes 1880072 | tf_op jit(solution)/shard_map/ppermute | solution.py:278
  3.6 6.2 %collective-permute-start.4 = (f32[12,8,12]{2,1,0:T(8,128)S(1)}, f32[12,8,12]{2,1,0:T(8,128)S(1)}, u32[]{:S(2)}, u32[]{:S(2)}) collective-permute-start(f32[12,8,12]{2,1,0:T(8,128)S(1)} %bitcast.8), channel_id=1, source_target_pairs={{0,7},{1,4},{2,5},{3,6},{4,1},{5,2},{6,3},{7,0},{8,9},{9,10},{10,1... | collective-permute-start | bytes 13832 | tf_op jit(solution)/shard_map/ppermute | solution.py:258
  5.8 10.1 %collective-permute-start.3 = (f32[12,8,12]{2,1,0:T(8,128)S(1)}, f32[12,8,12]{2,1,0:T(8,128)S(1)}, u32[]{:S(2)}, u32[]{:S(2)}) collective-permute-start(f32[12,8,12]{2,1,0:T(8,128)S(1)} %bitcast.9), channel_id=1, source_target_pairs={{0,2},{1,3},{2,0},{3,1},{4,6},{5,7},{6,4},{7,5},{8,10},{9,11},{10,... | collective-permute-start | bytes 13832 | tf_op jit(solution)/shard_map/ppermute | solution.py:280
  6.2 9.8 %collective-permute-start.2 = (f32[12,8,12]{2,1,0:T(8,128)S(1)}, f32[12,8,12]{2,1,0:T(8,128)S(1)}, u32[]{:S(2)}, u32[]{:S(2)}) collective-permute-start(f32[12,8,12]{2,1,0:T(8,128)S(1)} %bitcast.10), channel_id=1, source_target_pairs={{0,3},{1,0},{2,1},{3,2},{4,5},{5,6},{6,7},{7,4},{8,11},{9,8},{10,9... | collective-permute-start | bytes 13832 | tf_op jit(solution)/shard_map/ppermute | solution.py:259

commit v2 on v1

--- a/solution.py
+++ b/solution.py
@@ -25,14 +25,18 @@
     return jnp.where(core == 0, row, ROWS - 1 - row)
 
 
-def pack_kernel(green, outer, fore, rear, sem):
+def pack_kernel(green, coupling, outer, fore, rear, flat, matrices, sem):
     core = lax.axis_index("energy") % 2
     copies = []
     for row in range(ROWS):
         target = fore.at[row] if row < 2 else rear.at[row - 2]
         copies.append(pltpu.make_async_copy(green.at[energy_of(row, core)], target, sem.at[row]))
-    for copy in copies:
-        copy.start()
+    copies.append(pltpu.make_async_copy(coupling, matrices, sem.at[ROWS]))
+    for place in (4, 0, 1, 2, 3):
+        copies[place].start()
+    copies[4].wait()
+    pieces = [matrices[orbital] for orbital in range(ORB)] + [jnp.zeros((ATOM, 2 * LANES - ORB * ORB), F32)]
+    flat[...] = jnp.concatenate(pieces, axis=-1)
     for row in range(2):
         copies[row].wait()
         outer[NBR * row : NBR * (row + 1)] = fore[row, :, :, 0:128]
@@ -89,8 +93,7 @@
             y[tile, pl.ds(96 * k + f, 8, stride=ORB)] = totals[k]
 
 
-def coupling_rows(block):
-    rows = jnp.concatenate([block[orbital] for orbital in range(ORB)] + [jnp.zeros((ATOM, 2 * LANES - ORB * ORB), F32)], axis=-1)
+def three_parts(rows):
     high = rows.astype(BF16).astype(F32)
     mid = (rows - high).astype(BF16).astype(F32)
     return high, mid, rows - high - mid
@@ -105,12 +108,13 @@
     return sums
 
 
-def sum_kernel(fore, rear, neighbours, freq, emit, absorb, sums, weights, chosen, indices):
+def left_kernel(fore, rear, near, neighbours, freq, emit, absorb, mine, sums, weights, chosen, atom_coef, z,
+                indices, every, natural, x):
     position = lax.axis_index("energy")
     core = position % 2
     weight = kernel_values(freq[...], emit[...], absorb[...], 1 - 2 * core)
     inside = jnp.where((position > 0) & (position < lax.axis_size("energy") - 1), 1.0, 0.0).astype(F32)
-    for place, value in enumerate((weight[1] * inside, weight[0] * inside, weight[3], weight[4])):
+    for place, value in enumerate((weight[1] * inside, weight[0] * inside)):
         weights[place] = jnp.broadcast_to(value, (8, LANES))
     indices[...] = jnp.zeros_like(indices)
     indices[:, 0:NBR] = neighbours[...].astype(F32)
@@ -129,38 +133,23 @@
     spots = (lax.broadcasted_iota(jnp.int32, (LANES, LANES), 0) & 31) == (lax.broadcasted_iota(jnp.int32, (LANES, LANES), 1) & 7)
     chosen[:, width : width + LANES] = spots.astype(F32).astype(BF16)
 
-    def step(j, _):
-        for sub in range(2):
-            values = [fore[0, 2 * j + sub], fore[1, 2 * j + sub], rear[0, 2 * j + sub], rear[1, 2 * j + sub]]
-            for row in range(ROWS):
-                total = None
-                for source in range(ROWS):
-                    if abs(source - row) <= OFF:
-                        term = weight[source - row + OFF] * values[source]
-                        total = term if total is None else total + term
-                sums[row, 2 * j + sub] = total
-        return 0
-
-    lax.fori_loop(0, NBR // 2, step, 0)
-
-
-def left_kernel(sums, weights, near, mine, chosen, atom_coef, z, every, natural, x):
     every[...] = jnp.zeros_like(every)
-    for place, part in enumerate(coupling_rows(mine)):
+    for place, part in enumerate(three_parts(mine[...])):
         every[32 * place : 32 * place + 8] = part
     columns = every[...].T[0 : ORB * ORB].astype(BF16)
-    atom_coef[...] = jnp.dot(columns, chosen[:, LANES * TILES : LANES * (TILES + 1)], preferred_element_type=F32)
-    first, second = weights[2][0:1, 0:1], weights[3][0:1, 0:1]
-
-    def step(j, _):
-        for sub in range(2):
-            place = 2 * j + sub
-            a, b = near[1, place], near[0, place]
-            natural[pl.ds(pl.multiple_of(8 * place, 8), 8)] = sums[2, place] + second * a
-            natural[pl.ds(pl.multiple_of(ROW + 8 * place, 8), 8)] = sums[3, place] + (first * a + second * b)
-        return 0
-
-    lax.fori_loop(0, NBR // 2, step, 0)
+    atom_coef[...] = jnp.dot(columns, chosen[:, width : width + LANES], preferred_element_type=F32)
+    for j in range(NBR):
+        values = [fore[0, j], fore[1, j], rear[0, j], rear[1, j], near[1, j], near[0, j]]
+        for row in range(ROWS):
+            total = None
+            for source in range(ROWS + OFF):
+                if abs(source - row) <= OFF:
+                    term = weight[source - row + OFF] * values[source]
+                    total = term if total is None else total + term
+            if row < 2:
+                sums[row, j] = total
+            else:
+                natural[ROW * (row - 2) + 8 * j : ROW * (row - 2) + 8 * j + 8] = total
     turn_in(0, natural, x)
     for tile in range(TILES):
         if tile + 1 < TILES:
@@ -169,22 +158,27 @@
 
 
 def sender(result, out, first_row, core, sem):
-    copies = [pltpu.make_async_copy(result.at[pl.ds(ROW * half, ROW)], out.at[energy_of(first_row + half, core)], sem.at[half]) for half in range(2)]
+    pieces = []
+    for tile in range(TILES):
+        for half in range(2):
+            low, high = max(LANES * tile, ROW * half), min(LANES * (tile + 1), ROW * (half + 1))
+            if low < high:
+                target = out.at[energy_of(first_row + half, core), pl.ds(low - ROW * half, high - low)]
+                pieces.append((tile, pltpu.make_async_copy(result.at[pl.ds(low, high - low)], target, sem.at[len(pieces)])))
 
     def after(tile):
-        if tile == 2:
-            copies[0].start()
-        if tile == TILES - 1:
-            copies[1].start()
-
-    return copies, after
+        for ready, piece in pieces:
+            if ready == tile:
+                piece.start()
+
+    return [piece for _, piece in pieces], after
 
 
 def right_kernel(z, chosen, mine, from_next, from_second, from_third, out, pair_coef, every, result, y, sem):
     position = lax.axis_index("energy")
     crossed = jnp.where((position == 1) | (position == lax.axis_size("energy") - 2), 1, 0)
     for place, block in ((0, mine), (1 + 2 * crossed, from_next), (2, from_second), (3 - 2 * crossed, from_third)):
-        for part, rows in enumerate(coupling_rows(block)):
+        for part, rows in enumerate(three_parts(block[...])):
             every[pl.ds(pl.multiple_of(32 * part + 8 * place, 8), 8)] = rows
     every[96:128] = jnp.zeros((32, 2 * LANES), F32)
     columns = every[...].T[0 : ORB * ORB].astype(BF16)
@@ -239,74 +233,70 @@
     vmem = pl.BlockSpec(memory_space=pltpu.VMEM)
     anywhere = pl.BlockSpec(memory_space=pl.ANY)
     green = jnp.transpose(green_blocks, (0, 2, 1, 3))
-    mine = jnp.transpose(coupling, (1, 0, 2))
+    outer, fore, rear, mine = pl.pallas_call(
+        pack_kernel,
+        out_shape=(shape((PACK, 8, LANES)), shape((2, NBR, ATOM, WIDTH)), shape((2, NBR, ATOM, WIDTH)), shape((ATOM, 2 * LANES))),
+        in_specs=[anywhere] * 2,
+        out_specs=(vmem,) * 4,
+        scratch_shapes=[pltpu.VMEM((ORB, ATOM, ORB), F32), pltpu.SemaphoreType.DMA((ROWS + 1,))],
+        compiler_params=pltpu.CompilerParams(vmem_limit_bytes=GRANT),
+        name="pack",
+    )(*(pltpu.with_memory_space_constraint(array, pltpu.HBM) for array in (green, jnp.transpose(coupling, (1, 0, 2)))))
+
     ends = {0: 1, energies - 1: energies - 2}
     others = {other: end for end, other in ends.items()}
     up, down = [], []
     for e in range(energies):
         for a in range(atoms):
             here, above, below = e * atoms + a, (a + 1) % atoms, (a - 1) % atoms
-            if e in ends:
+            if e in ends and a % 2:
                 up.append((here, ends[e] * atoms + below))
                 down.append((here, e * atoms + below))
-            elif e in others:
+            elif e in ends:
+                up.append((here, e * atoms + above))
+                down.append((here, ends[e] * atoms + above))
+            elif e in others and a % 2:
                 up.append((here, others[e] * atoms + above))
                 down.append((here, e * atoms + above))
+            elif e in others:
+                up.append((here, e * atoms + below))
+                down.append((here, others[e] * atoms + below))
             else:
                 up.append((here, e * atoms + above))
                 down.append((here, e * atoms + below))
     third = lax.ppermute(mine, ("energy", "atom"), up)
     first = lax.ppermute(mine, ("energy", "atom"), down)
-    outer, fore, rear = pl.pallas_call(
-        pack_kernel,
-        out_shape=(shape((PACK, 8, LANES)), shape((2, NBR, ATOM, WIDTH)), shape((2, NBR, ATOM, WIDTH))),
-        in_specs=[pl.BlockSpec(memory_space=pltpu.HBM)],
-        out_specs=(vmem, vmem, vmem),
-        scratch_shapes=[pltpu.SemaphoreType.DMA((ROWS,))],
-        compiler_params=pltpu.CompilerParams(vmem_limit_bytes=GRANT),
-        name="pack",
-    )(pltpu.with_memory_space_constraint(green, pltpu.HBM))
-
     pairs = []
     for e in range(energies):
         for a in range(atoms):
             if e in (0, energies - 1):
-                to = e * atoms + (a + 1) % atoms
+                to = e * atoms + atoms - 1 - a
             else:
                 to = (e + 1 if e % 2 else e - 1) * atoms + a
             pairs.append((e * atoms + a, to))
     far = lax.ppermute(outer, ("energy", "atom"), pairs)
     near = lax.ppermute(rear, "energy", [(e, e ^ 1) for e in range(energies)])
     second = lax.ppermute(mine, "atom", [(a, (a + 2) % atoms) for a in range(atoms)])
-    sums, weights, chosen = pl.pallas_call(
-        sum_kernel,
-        out_shape=(shape((ROWS, NBR, ATOM, WIDTH)), shape((4, 8, LANES)), shape((LANES, (TILES + 1) * LANES), BF16)),
-        in_specs=[vmem] * 6,
-        out_specs=(vmem, vmem, vmem),
-        scratch_shapes=[pltpu.VMEM((ATOM, LANES), F32)],
-        compiler_params=pltpu.CompilerParams(vmem_limit_bytes=GRANT),
-        name="sums",
-    )(fore, rear, neighbours, freq_offset[None], emit_weight[None], absorb_weight[None])
     turned = pltpu.VMEM((TILES, WIDTH, LANES), F32)
     halfway = shape((TILES, 2 * WIDTH, LANES))
     rowwise = pltpu.VMEM((TILES * LANES, WIDTH), F32)
     table = pltpu.VMEM((LANES, 2 * LANES), F32)
     rows = jax.ShapeDtypeStruct((ROWS, ROW, WIDTH), F32)
-    atom_coef, z = pl.pallas_call(
+    sums, weights, chosen, atom_coef, z = pl.pallas_call(
         left_kernel,
-        out_shape=(shape((ORB * ORB, LANES)), halfway),
-        in_specs=[vmem] * 5,
-        out_specs=(vmem, vmem),
-        scratch_shapes=[table, rowwise, turned],
+        out_shape=(shape((2, NBR, ATOM, WIDTH)), shape((2, 8, LANES)), shape((LANES, (TILES + 1) * LANES), BF16), shape((ORB * ORB, LANES)), halfway),
+        in_specs=[vmem] * 8,
+        out_specs=(vmem,) * 5,
+        scratch_shapes=[pltpu.VMEM((ATOM, LANES), F32), table, rowwise, turned],
         compiler_params=pltpu.CompilerParams(vmem_limit_bytes=GRANT),
         name="left",
-    )(*map(held, (sums, weights, near, mine, chosen)))
+    )(*map(held, (fore, rear, near)), neighbours, freq_offset[None], emit_weight[None], absorb_weight[None], held(mine))
     begun, pair_coef = pl.pallas_call(
         right_kernel,
         out_shape=(rows, shape((TILES, ORB * ORB, LANES))),
         in_specs=[vmem] * 6,
         out_specs=(anywhere, vmem),
-        scratch_shapes=[table, rowwise, turned, pltpu.SemaphoreType.DMA((2,))],
+        scratch_shapes=[table, rowwise, turned, pltpu.SemaphoreType.DMA((TILES + 1,))],
         compiler_params=pltpu.CompilerParams(vmem_limit_bytes=GRANT),
         name="right",
     )(*map(held, (z, chosen, mine, first, second, third)))
@@ -315,7 +305,7 @@
         out_shape=rows,
         in_specs=[vmem] * 5 + [anywhere],
         out_specs=anywhere,
-        scratch_shapes=[rowwise, rowwise, turned, halfway, turned, pltpu.SemaphoreType.DMA((2,))],
+        scratch_shapes=[rowwise, rowwise, turned, halfway, turned, pltpu.SemaphoreType.DMA((TILES + 1,))],
         input_output_aliases={5: 0},
         compiler_params=pltpu.CompilerParams(vmem_limit_bytes=GRANT),
         name="last",

time: 21 us -> 18.2 us (0.87)
  the two profiles are of different devices: /device:TPU:231 before, /device:TPU:224 now
where the time goes in v2:
time: 18.2 us; the launch traced here: 18.1 us
  starting transfers between devices  8.01 us (44%)
  Pallas kernels  7.45 us (41%)
  waiting for transfers between devices  2.51 us (14%)
    ppermute x1, starting transfers between devices, planned(): far = lax.ppermute(outer, ('energy', 'atom'), pairs)  3.3 us
    ppermute x1, starting transfers between devices, planned(): first = lax.ppermute(mine, ('energy', 'atom'), down)  3.01 us
    pallas_call x1, Pallas kernels, planned(): pl.pallas_call(last_kernel, out_shape=rows, in_specs=[vmem] * 5 + [anywhe...  2.59 us
    ppermute x1, waiting for transfers between devices, planned(): lax.ppermute(mine, 'atom', [(a, (a + 2) % atoms) for a in range(atoms)])  2.17 us
    pallas_call x1, Pallas kernels, planned(): pl.pallas_call(right_kernel, out_shape=(rows, shape((TILES, ORB * ORB, LA...  2.03 us
    pallas_call x1, Pallas kernels, planned(): pl.pallas_call(pack_kernel, out_shape=(shape((PACK, 8, LANES)), shape((2,...  1.5 us
    pallas_call x1, Pallas kernels, planned(): pl.pallas_call(left_kernel, out_shape=(shape((2, NBR, ATOM, WIDTH)), shap...  1.34 us
    ppermute x1, starting transfers between devices, planned(): third = lax.ppermute(mine, ('energy', 'atom'), up)  0.97 us
  transfers between devices with their start and end apart: 5, of which 2 were waited for; matrix products, arithmetic and copies ran while one was open for 0% of the time, Pallas kernels for 19%

profile of v2, /device:TPU:224, one launch (start us, length us, event | category | flops | bytes accessed | tf_op | source)
XLA Modules:
  0.0 18.1 jit_solution(18070636204700990669)
XLA Ops:
  0.0 0.0 copy-start
  0.0 0.0 copy-start.1
  0.0 0.0 copy-start.2
  0.0 0.0 copy-start.3
  0.0 1.5 %pack.1 = (f32[153,8,128]{2,1,0:T(8,128)S(1)}, f32[2,34,8,288]{3,2,1,0:T(8,128)S(1)}, f32[2,34,8,288]{3,2,1,0:T(8,128)S(1)}, f32[8,256]{1,0:T(8,128)S(1)}) custom-call(f32[4,34,8,288]{3,2,1,0:T(8,128)} %bitcast.11, f32[12,8,12]{2,1,0:T(8,128)} %bitcast.12), custom_call_target="tpu_custom_call" | custom-call | tf_op jit(solution)/shard_map/pack/pallas_call | solution.py:236
  1.5 0.1 collective-permute-start.1
  1.6 3.3 %collective-permute-start = (f32[153,8,128]{2,1,0:T(8,128)S(1)}, f32[153,8,128]{2,1,0:T(8,128)S(1)}, u32[]{:S(2)}, u32[]{:S(2)}) collective-permute-start(f32[153,8,128]{2,1,0:T(8,128)S(1)} %get-tuple-element.16), channel_id=1, source_target_pairs={{0,3},{1,2},{2,1},{3,0},{4,8},{5,9},{6,10},{7,11},{8,4},{9,5},{10,... | collective-permute-start | bytes 1880072 | tf_op jit(solution)/shard_map/ppermute | solution.py:277
  4.9 3.0 %collective-permute-start.2 = (f32[8,256]{1,0:T(8,128)S(1)}, f32[8,256]{1,0:T(8,128)S(1)}, u32[]{:S(2)}, u32[]{:S(2)}) collective-permute-start(f32[8,256]{1,0:T(8,128)S(1)} %get-tuple-element.19.mine), channel_id=1, source_target_pairs={{0,5},{1,0},{2,7},{3,2},{4,3},{5,6},{6,1},{7,4},{8,11},{9,8},{10,9... | collective-permute-start | bytes 24584 | tf_op jit(solution)/shard_map/ppermute | solution.py:268
  7.9 0.6 %collective-permute-start.3 = (f32[8,256]{1,0:T(8,128)S(1)}, f32[8,256]{1,0:T(8,128)S(1)}, u32[]{:S(2)}, u32[]{:S(2)}) collective-permute-start(f32[8,256]{1,0:T(8,128)S(1)} %get-tuple-element.19.mine), channel_id=1, source_target_pairs={{0,2},{1,3},{2,0},{3,1},{4,6},{5,7},{6,4},{7,5},{8,10},{9,11},{10,... | collective-permute-start | bytes 24584 | tf_op jit(solution)/shard_map/ppermute | solution.py:279
  8.6 1.0 %collective-permute-start.4 = (f32[8,256]{1,0:T(8,128)S(1)}, f32[8,256]{1,0:T(8,128)S(1)}, u32[]{:S(2)}, u32[]{:S(2)}) collective-permute-start(f32[8,256]{1,0:T(8,128)S(1)} %get-tuple-element.19.mine), channel_id=1, source_target_pairs={{0,1},{1,4},{2,3},{3,6},{4,7},{5,2},{6,5},{7,0},{8,9},{9,10},{10,1... | collective-permute-start | bytes 24584 | tf_op jit(solution)/shard_map/ppermute | solution.py:267
  9.5 0.0 collective-permute-done.1.near
  9.5 0.0 copy-done
  9.6 0.0 copy-done.1
  9.6 0.0 copy-done.2
  9.6 0.0 copy-done.3
  9.6 1.3 %left.1 = (f32[2,34,8,288]{3,2,1,0:T(8,128)S(1)}, f32[2,8,128]{2,1,0:T(8,128)S(1)}, bf16[128,768]{1,0:T(8,128)(2,1)S(1)}, f32[144,128]{1,0:T(8,128)S(1)}, f32[5,576,128]{2,1,0:T(8,128)S(1)}) custom-call(f32[2,34,8,288]{3,2,1,0:T(8,128)S(1)} %get-tuple-element.17.fore, f32[2,34,8,288]{3,2,1,0:T(8,128)S(1)} %get-tuple-element.18.rear, ...), custom_call_target="tpu_custom_call" | custom-call | tf_op jit(solution)/shard_map/left/pallas_call | solution.py:285
  10.9 0.0 collective-permute-done.2.from_next
  10.9 2.2 %collective-permute-done.3.from_second = f32[8,256]{1,0:T(8,128)S(1)} collective-permute-done((f32[8,256]{1,0:T(8,128)S(1)}, f32[8,256]{1,0:T(8,128)S(1)}, u32[]{:S(2)}, u32[]{:S(2)}) %collective-permute-start.3) | collective-permute-done | bytes 8224 | tf_op jit(solution)/shard_map/ppermute | solution.py:279
  13.1 0.3 %collective-permute-done.4.from_third = f32[8,256]{1,0:T(8,128)S(1)} collective-permute-done((f32[8,256]{1,0:T(8,128)S(1)}, f32[8,256]{1,0:T(8,128)S(1)}, u32[]{:S(2)}, u32[]{:S(2)}) %collective-permute-start.4) | collective-permute-done | bytes 8224 | tf_op jit(solution)/shard_map/ppermute | solution.py:267
  13.4 2.0 %right.1 = (f32[4,272,288]{2,1,0:T(8,128)}, f32[5,144,128]{2,1,0:T(8,128)S(1)}) custom-call(f32[5,576,128]{2,1,0:T(8,128)S(1)} %get-tuple-element.21.z, bf16[128,768]{1,0:T(8,128)(2,1)S(1)} %get-tuple-element.22.chosen, f32[8,256]{1,0:T(8,128)S(1)} %get-tuple-element.19.mine, f32[8,256]{1,0:T(8,128)S(1)} %collective-permute-done.2.from_next, ...), custom_call_target="tpu_custom_call" | custom-call | tf_op jit(solution)/shard_map/right/pallas_call | solution.py:294
  15.5 0.0 collective-permute-done.outer
  15.5 2.6 %last.1 = f32[4,272,288]{2,1,0:T(8,128)} custom-call(f32[153,8,128]{2,1,0:T(8,128)S(1)} %collective-permute-done.outer, f32[2,34,8,288]{3,2,1,0:T(8,128)S(1)} %get-tuple-element.20.sums, f32[5,144,128]{2,1,0:T(8,128)S(1)} %get-tuple-element.23.pair_coef, f32[144,128]{1,0:T(8,128)S(1)} %get-tuple-element.24.atom_coef, ...), custom_call_target="tpu_custom_call", output_to_operand_aliasing={{}: (5, {})} | custom-call | tf_op jit(solution)/shard_map/last/pallas_call | solution.py:303
Async XLA Ops:
  0.0 9.6 %copy-start = (s32[8,34]{1,0:T(8,128)S(1)}, s32[8,34]{1,0:T(8,128)}, u32[]{:S(2)}) copy-start(s32[8,34]{1,0:T(8,128)} %neighbours.1) | copy-start | bytes 3268
  0.0 9.6 %copy-start.1 = (s32[64]{0:T(128)S(1)}, s32[64]{0:T(128)}, u32[]{:S(2)}) copy-start(s32[64]{0:T(128)} %param.9) | copy-start | bytes 772
  0.0 9.6 %copy-start.2 = (f32[64]{0:T(128)S(1)}, f32[64]{0:T(128)}, u32[]{:S(2)}) copy-start(f32[64]{0:T(128)} %param.10) | copy-start | bytes 772
  0.0 9.6 %copy-start.3 = (f32[64]{0:T(128)S(1)}, f32[64]{0:T(128)}, u32[]{:S(2)}) copy-start(f32[64]{0:T(128)} %param.11) | copy-start | bytes 772
  1.5 8.0 %collective-permute-start.1 = (f32[2,34,8,288]{3,2,1,0:T(8,128)S(1)}, f32[2,34,8,288]{3,2,1,0:T(8,128)S(1)}, u32[]{:S(2)}, u32[]{:S(2)}) collective-permute-start(f32[2,34,8,288]{3,2,1,0:T(8,128)S(1)} %get-tuple-element.18.rear), channel_id=1, source_target_pairs={{0,4},{4,0},{8,12},{12,8},{16,20},{20,16},{24,28},{28,24},{32,36},... | collective-permute-start | bytes 1880072 | tf_op jit(solution)/shard_map/ppermute | solution.py:278
  1.6 13.8 %collective-permute-start = (f32[153,8,128]{2,1,0:T(8,128)S(1)}, f32[153,8,128]{2,1,0:T(8,128)S(1)}, u32[]{:S(2)}, u32[]{:S(2)}) collective-permute-start(f32[153,8,128]{2,1,0:T(8,128)S(1)} %get-tuple-element.16), channel_id=1, source_target_pairs={{0,3},{1,2},{2,1},{3,0},{4,8},{5,9},{6,10},{7,11},{8,4},{9,5},{10,... | collective-permute-start | bytes 1880072 | tf_op jit(solution)/shard_map/ppermute | solution.py:277
  4.9 6.0 %collective-permute-start.2 = (f32[8,256]{1,0:T(8,128)S(1)}, f32[8,256]{1,0:T(8,128)S(1)}, u32[]{:S(2)}, u32[]{:S(2)}) collective-permute-start(f32[8,256]{1,0:T(8,128)S(1)} %get-tuple-element.19.mine), channel_id=1, source_target_pairs={{0,5},{1,0},{2,7},{3,2},{4,3},{5,6},{6,1},{7,4},{8,11},{9,8},{10,9... | collective-permute-start | bytes 24584 | tf_op jit(solution)/shard_map/ppermute | solution.py:268
  7.9 5.2 %collective-permute-start.3 = (f32[8,256]{1,0:T(8,128)S(1)}, f32[8,256]{1,0:T(8,128)S(1)}, u32[]{:S(2)}, u32[]{:S(2)}) collective-permute-start(f32[8,256]{1,0:T(8,128)S(1)} %get-tuple-element.19.mine), channel_id=1, source_target_pairs={{0,2},{1,3},{2,0},{3,1},{4,6},{5,7},{6,4},{7,5},{8,10},{9,11},{10,... | collective-permute-start | bytes 24584 | tf_op jit(solution)/shard_map/ppermute | solution.py:279
  8.6 4.9 %collective-permute-start.4 = (f32[8,256]{1,0:T(8,128)S(1)}, f32[8,256]{1,0:T(8,128)S(1)}, u32[]{:S(2)}, u32[]{:S(2)}) collective-permute-start(f32[8,256]{1,0:T(8,128)S(1)} %get-tuple-element.19.mine), channel_id=1, source_target_pairs={{0,1},{1,4},{2,3},{3,6},{4,7},{5,2},{6,5},{7,0},{8,9},{9,10},{10,1... | collective-permute-start | bytes 24584 | tf_op jit(solution)/shard_map/ppermute | solution.py:267

commit v3 on v2

--- a/solution.py
+++ b/solution.py
@@ -47,50 +47,59 @@
     copies[3].wait()
 
 
+def filled(tile):
+    return min(LANES, 2 * ROW - LANES * tile)
+
+
 def turn_in(tile, natural, x):
-    rows = slice(LANES * tile, LANES * (tile + 1))
-    x[tile, 0:128] = natural[rows, 0:128].T
-    x[tile, 128:256] = natural[rows, 128:256].T
-    x[tile, 256:288] = natural[rows, 256:288].T
+    size = filled(tile)
+    rows = slice(LANES * tile, LANES * tile + size)
+    x[tile, 0:128, 0:size] = natural[rows, 0:128].T
+    x[tile, 128:256, 0:size] = natural[rows, 128:256].T
+    x[tile, 256:288, 0:size] = natural[rows, 256:288].T
 
 
 def turn_out(tile, result, y):
-    rows = slice(LANES * tile, LANES * (tile + 1))
-    result[rows, 0:128] = y[tile, 0:128].T
-    result[rows, 128:256] = y[tile, 128:256].T
-    result[rows, 256:288] = y[tile, 256:288].T
+    size = filled(tile)
+    rows = slice(LANES * tile, LANES * tile + size)
+    result[rows, 0:128] = y[tile, 0:128, 0:size].T
+    result[rows, 128:256] = y[tile, 128:256, 0:size].T
+    result[rows, 256:288] = y[tile, 256:288, 0:size].T
+
+
+def blocks_of(tile):
+    return [divmod(block, NBR) for block in range(16 * tile, 16 * tile + filled(tile) // 8)]
 
 
 def left(tile, atom_coef, x, z):
     low = lax.broadcasted_iota(jnp.int32, (8, LANES), 0) < 4
-    for a in range(ORB):
-        totals = [[None] * 3 for _ in range(2)]
+    for block in range(0, ORB, 6):
+        totals = {}
         for pair in range(6):
-            first = jnp.broadcast_to(atom_coef[ORB * a + 2 * pair : ORB * a + 2 * pair + 1], (8, LANES))
-            last = jnp.broadcast_to(atom_coef[ORB * a + 2 * pair + 1 : ORB * a + 2 * pair + 2], (8, LANES))
-            coef = (first, jnp.where(low, first, last), last)
-            for part in range(2):
-                for k in range(3):
-                    term = coef[k] * x[tile, pl.ds(144 * part + 24 * pair + 8 * k, 8)]
-                    totals[part][k] = term if pair == 0 else totals[part][k] + term
-        for part in range(2):
-            for k in range(3):
-                z[tile, pl.ds((ORB * part + a) * 24 + 8 * k, 8)] = totals[part][k]
+            values = [[x[tile, pl.ds(144 * part + 24 * pair + 8 * k, 8)] for k in range(3)] for part in range(2)]
+            for a in range(block, block + 6):
+                first = jnp.broadcast_to(atom_coef[ORB * a + 2 * pair : ORB * a + 2 * pair + 1], (8, LANES))
+                last = jnp.broadcast_to(atom_coef[ORB * a + 2 * pair + 1 : ORB * a + 2 * pair + 2], (8, LANES))
+                coef = (first, jnp.where(low, first, last), last)
+                for part in range(2):
+                    for k in range(3):
+                        term = coef[k] * values[part][k]
+                        totals[a, part, k] = term if pair == 0 else totals[a, part, k] + term
+        for (a, part, k), total in totals.items():
+            z[tile, pl.ds((ORB * part + a) * 24 + 8 * k, 8)] = total
 
 
 def right(tile, pair_coef, z, y):
-    values = []
+    totals = {}
     for d in range(ORB):
-        values.append([z[tile, pl.ds(192 * k + d, 8, stride=24)] + z[tile, pl.ds(192 * k + 12 + d, 8, stride=24)] for k in range(3)])
-    for f in range(ORB):
-        totals = [None] * 3
-        for d in range(ORB):
+        values = [z[tile, pl.ds(192 * k + d, 8, stride=24)] + z[tile, pl.ds(192 * k + 12 + d, 8, stride=24)] for k in range(3)]
+        for f in range(ORB):
             coef = jnp.broadcast_to(pair_coef[tile, ORB * f + d : ORB * f + d + 1], (8, LANES))
             for k in range(3):
-                term = coef * values[d][k]
-                totals[k] = term if d == 0 else totals[k] + term
-        for k in range(3):
-            y[tile, pl.ds(96 * k + f, 8, stride=ORB)] = totals[k]
+                term = coef * values[k]
+                totals[f, k] = term if d == 0 else totals[f, k] + term
+    for (f, k), total in totals.items():
+        y[tile, pl.ds(96 * k + f, 8, stride=ORB)] = total
 
 
 def three_parts(rows):
@@ -138,22 +147,26 @@
         every[32 * place : 32 * place + 8] = part
     columns = every[...].T[0 : ORB * ORB].astype(BF16)
     atom_coef[...] = jnp.dot(columns, chosen[:, width : width + LANES], preferred_element_type=F32)
-    for j in range(NBR):
-        values = [fore[0, j], fore[1, j], rear[0, j], rear[1, j], near[1, j], near[0, j]]
-        for row in range(ROWS):
-            total = None
-            for source in range(ROWS + OFF):
-                if abs(source - row) <= OFF:
-                    term = weight[source - row + OFF] * values[source]
-                    total = term if total is None else total + term
-            if row < 2:
-                sums[row, j] = total
-            else:
-                natural[ROW * (row - 2) + 8 * j : ROW * (row - 2) + 8 * j + 8] = total
-    turn_in(0, natural, x)
+    sources = [(fore, 0), (fore, 1), (rear, 0), (rear, 1), (near, 1), (near, 0)]
+
+    def energy_sum(row, j):
+        total = None
+        for source in range(max(0, row - OFF), min(ROWS + OFF, row + OFF + 1)):
+            ref, place = sources[source]
+            term = weight[source - row + OFF] * ref[place, j]
+            total = term if total is None else total + term
+        return total
+
+    def prepare(tile):
+        for row, j in blocks_of(tile):
+            natural[ROW * row + 8 * j : ROW * row + 8 * j + 8] = energy_sum(2 + row, j)
+            sums[row, j] = energy_sum(row, j)
+        turn_in(tile, natural, x)
+
+    prepare(0)
     for tile in range(TILES):
         if tile + 1 < TILES:
-            turn_in(tile + 1, natural, x)
+            prepare(tile + 1)
         left(tile, atom_coef, x, z)
 
 
@@ -174,7 +187,7 @@
     return [piece for _, piece in pieces], after
 
 
-def right_kernel(z, chosen, mine, from_next, from_second, from_third, out, pair_coef, every, result, y, sem):
+def right_kernel(z, chosen, mine, from_next, from_second, from_third, result, pair_coef, every, y):
     position = lax.axis_index("energy")
     crossed = jnp.where((position == 1) | (position == lax.axis_size("energy") - 2), 1, 0)
     for place, block in ((0, mine), (1 + 2 * crossed, from_next), (2, from_second), (3 - 2 * crossed, from_third)):
@@ -184,42 +197,46 @@
     columns = every[...].T[0 : ORB * ORB].astype(BF16)
     for tile in range(TILES):
         pair_coef[tile] = jnp.dot(columns, chosen[:, LANES * tile : LANES * (tile + 1)], preferred_element_type=F32)
-    copies, after = sender(result, out, 2, lax.axis_index("energy") % 2, sem)
     for tile in range(TILES):
         right(tile, pair_coef, z, y)
         turn_out(tile, result, y)
-        after(tile)
-    for copy in copies:
-        copy.wait()
-
-
-def last_kernel(outer, sums, pair_coef, atom_coef, weights, begun, out, natural, result, x, z, y, sem):
+
+
+def last_kernel(outer, sums, pair_coef, atom_coef, weights, done, out, natural, result, x, z, y, sem):
+    core = lax.axis_index("energy") % 2
+    finished = [pltpu.make_async_copy(done.at[pl.ds(ROW * half, ROW)], out.at[energy_of(2 + half, core)], sem.at[TILES + 1 + half]) for half in range(2)]
+    for copy in finished:
+        copy.start()
     near, far = weights[0], weights[1]
-    for half in range(2):
-        a = outer[2 * NBR * half : 2 * NBR * half + NBR]
-        b = outer[2 * NBR * half + NBR : 2 * NBR * half + 2 * NBR]
-        lanes = slice(128 * half, 128 * half + 128)
-        natural[0:ROW, lanes] = (sums[0, :, :, lanes] + (near * a + far * b)).reshape(ROW, LANES)
-        natural[ROW : 2 * ROW, lanes] = (sums[1, :, :, lanes] + far * a).reshape(ROW, LANES)
-    near_part, far_part = near[0:1, 0:32], far[0:1, 0:32]
-    for half in range(2):
-        a = outer[4 * NBR : PACK, :, 32 * half : 32 * half + 32]
-        b = outer[4 * NBR : PACK, :, 64 + 32 * half : 96 + 32 * half]
-        rows = slice(TAIL * 8 * half, TAIL * 8 * (half + 1))
-        tiles = slice(TAIL * half, TAIL * (half + 1))
-        natural[rows, 256:288] = (sums[0, tiles, :, 256:288] + (near_part * a + far_part * b)).reshape(TAIL * 8, 32)
-        rows = slice(ROW + TAIL * 8 * half, ROW + TAIL * 8 * (half + 1))
-        natural[rows, 256:288] = (sums[1, tiles, :, 256:288] + far_part * a).reshape(TAIL * 8, 32)
-    copies, after = sender(result, out, 0, lax.axis_index("energy") % 2, sem)
-    turn_in(0, natural, x)
+    near_part, far_part = near[:, 0:32], far[:, 0:32]
+
+    def prepare(tile):
+        for row, j in blocks_of(tile):
+            rows = slice(ROW * row + 8 * j, ROW * row + 8 * j + 8)
+            first = far if row else near
+            for half in range(2):
+                lanes = slice(128 * half, 128 * half + 128)
+                total = sums[row, j, :, lanes] + first * outer[2 * NBR * half + j]
+                if row == 0:
+                    total = total + far * outer[2 * NBR * half + NBR + j]
+                natural[rows, lanes] = total
+            part, place = divmod(j, TAIL)
+            total = sums[row, j, :, 256:288] + (far_part if row else near_part) * outer[4 * NBR + place, :, 32 * part : 32 * part + 32]
+            if row == 0:
+                total = total + far_part * outer[4 * NBR + place, :, 64 + 32 * part : 96 + 32 * part]
+            natural[rows, 256:288] = total
+        turn_in(tile, natural, x)
+
+    copies, after = sender(result, out, 0, core, sem)
+    prepare(0)
     for tile in range(TILES):
         if tile + 1 < TILES:
-            turn_in(tile + 1, natural, x)
+            prepare(tile + 1)
         left(tile, atom_coef, x, z)
         right(tile, pair_coef, z, y)
         turn_out(tile, result, y)
         after(tile)
-    for copy in copies:
+    for copy in finished + copies:
         copy.wait()
 
 
@@ -291,25 +308,24 @@
         compiler_params=pltpu.CompilerParams(vmem_limit_bytes=GRANT),
         name="left",
     )(*map(held, (fore, rear, near)), neighbours, freq_offset[None], emit_weight[None], absorb_weight[None], held(mine))
-    begun, pair_coef = pl.pallas_call(
+    done, pair_coef = pl.pallas_call(
         right_kernel,
-        out_shape=(rows, shape((TILES, ORB * ORB, LANES))),
+        out_shape=(shape((2 * ROW, WIDTH)), shape((TILES, ORB * ORB, LANES))),
         in_specs=[vmem] * 6,
-        out_specs=(anywhere, vmem),
-        scratch_shapes=[table, rowwise, turned, pltpu.SemaphoreType.DMA((TILES + 1,))],
+        out_specs=(vmem, vmem),
+        scratch_shapes=[table, turned],
         compiler_params=pltpu.CompilerParams(vmem_limit_bytes=GRANT),
         name="right",
     )(*map(held, (z, chosen, mine, first, second, third)))
     out = pl.pallas_call(
         last_kernel,
         out_shape=rows,
-        in_specs=[vmem] * 5 + [anywhere],
+        in_specs=[vmem] * 6,
         out_specs=anywhere,
-        scratch_shapes=[rowwise, rowwise, turned, halfway, turned, pltpu.SemaphoreType.DMA((TILES + 1,))],
-        input_output_aliases={5: 0},
+        scratch_shapes=[rowwise, rowwise, turned, halfway, turned, pltpu.SemaphoreType.DMA((TILES + 3,))],
         compiler_params=pltpu.CompilerParams(vmem_limit_bytes=GRANT),
         name="last",
-    )(*map(held, (far, sums, pair_coef, atom_coef, weights)), begun)
+    )(*map(held, (far, sums, pair_coef, atom_coef, weights, done)))
     return jnp.transpose(out.reshape(ROWS, NBR, ATOM, WIDTH), (0, 2, 1, 3))
 
 

time: 18.2 us -> 18.1 us (level)
  the two profiles are of different devices: /device:TPU:224 before, /device:TPU:103 now
where the time goes in v3:
time: 18.1 us; the launch traced here: 18 us
  starting transfers between devices  7.29 us (40%)
  Pallas kernels  6.8 us (38%)
  waiting for transfers between devices  3.81 us (21%)
    ppermute x1, starting transfers between devices, planned(): far = lax.ppermute(outer, ('energy', 'atom'), pairs)  2.75 us
    ppermute x1, starting transfers between devices, planned(): first = lax.ppermute(mine, ('energy', 'atom'), down)  2.73 us
    pallas_call x1, Pallas kernels, planned(): pl.pallas_call(last_kernel, out_shape=rows, in_specs=[vmem] * 6, out_spec...  2.66 us
    ppermute x1, waiting for transfers between devices, planned(): far = lax.ppermute(outer, ('energy', 'atom'), pairs)  2.21 us
    ppermute x1, waiting for transfers between devices, planned(): lax.ppermute(mine, 'atom', [(a, (a + 2) % atoms) for a in range(atoms)])  1.5 us
    pallas_call x1, Pallas kernels, planned(): pl.pallas_call(pack_kernel, out_shape=(shape((PACK, 8, LANES)), shape((2,...  1.5 us
    pallas_call x1, Pallas kernels, planned(): pl.pallas_call(left_kernel, out_shape=(shape((2, NBR, ATOM, WIDTH)), shap...  1.41 us
    pallas_call x1, Pallas kernels, planned(): pl.pallas_call(right_kernel, out_shape=(shape((2 * ROW, WIDTH)), shape((T...  1.23 us
  transfers between devices with their start and end apart: 5, of which 3 were waited for; matrix products, arithmetic and copies ran while one was open for 0% of the time, Pallas kernels for 15%

profile of v3, /device:TPU:103, one launch (start us, length us, event | category | flops | bytes accessed | tf_op | source)
XLA Modules:
  0.0 18.0 jit_solution(17244133234349015924)
XLA Ops:
  0.0 0.0 copy-start
  0.0 0.0 copy-start.1
  0.0 0.0 copy-start.2
  0.0 0.0 copy-start.3
  0.0 1.5 %pack.1 = (f32[153,8,128]{2,1,0:T(8,128)S(1)}, f32[2,34,8,288]{3,2,1,0:T(8,128)S(1)}, f32[2,34,8,288]{3,2,1,0:T(8,128)S(1)}, f32[8,256]{1,0:T(8,128)S(1)}) custom-call(f32[4,34,8,288]{3,2,1,0:T(8,128)} %bitcast.11, f32[12,8,12]{2,1,0:T(8,128)} %bitcast.12), custom_call_target="tpu_custom_call" | custom-call | tf_op jit(solution)/shard_map/pack/pallas_call | solution.py:253
  1.5 0.8 %collective-permute-start.1 = (f32[2,34,8,288]{3,2,1,0:T(8,128)S(1)}, f32[2,34,8,288]{3,2,1,0:T(8,128)S(1)}, u32[]{:S(2)}, u32[]{:S(2)}) collective-permute-start(f32[2,34,8,288]{3,2,1,0:T(8,128)S(1)} %get-tuple-element.18.rear), channel_id=1, source_target_pairs={{0,4},{4,0},{8,12},{12,8},{16,20},{20,16},{24,28},{28,24},{32,36},... | collective-permute-start | bytes 1880072 | tf_op jit(solution)/shard_map/ppermute | solution.py:295
  2.3 2.7 %collective-permute-start = (f32[153,8,128]{2,1,0:T(8,128)S(1)}, f32[153,8,128]{2,1,0:T(8,128)S(1)}, u32[]{:S(2)}, u32[]{:S(2)}) collective-permute-start(f32[153,8,128]{2,1,0:T(8,128)S(1)} %get-tuple-element.16), channel_id=1, source_target_pairs={{0,3},{1,2},{2,1},{3,0},{4,8},{5,9},{6,10},{7,11},{8,4},{9,5},{10,... | collective-permute-start | bytes 1880072 | tf_op jit(solution)/shard_map/ppermute | solution.py:294
  5.0 2.7 %collective-permute-start.2 = (f32[8,256]{1,0:T(8,128)S(1)}, f32[8,256]{1,0:T(8,128)S(1)}, u32[]{:S(2)}, u32[]{:S(2)}) collective-permute-start(f32[8,256]{1,0:T(8,128)S(1)} %get-tuple-element.19.mine), channel_id=1, source_target_pairs={{0,5},{1,0},{2,7},{3,2},{4,3},{5,6},{6,1},{7,4},{8,11},{9,8},{10,9... | collective-permute-start | bytes 24584 | tf_op jit(solution)/shard_map/ppermute | solution.py:285
  7.8 0.3 %collective-permute-start.3 = (f32[8,256]{1,0:T(8,128)S(1)}, f32[8,256]{1,0:T(8,128)S(1)}, u32[]{:S(2)}, u32[]{:S(2)}) collective-permute-start(f32[8,256]{1,0:T(8,128)S(1)} %get-tuple-element.19.mine), channel_id=1, source_target_pairs={{0,2},{1,3},{2,0},{3,1},{4,6},{5,7},{6,4},{7,5},{8,10},{9,11},{10,... | collective-permute-start | bytes 24584 | tf_op jit(solution)/shard_map/ppermute | solution.py:296
  8.1 0.7 %collective-permute-start.4 = (f32[8,256]{1,0:T(8,128)S(1)}, f32[8,256]{1,0:T(8,128)S(1)}, u32[]{:S(2)}, u32[]{:S(2)}) collective-permute-start(f32[8,256]{1,0:T(8,128)S(1)} %get-tuple-element.19.mine), channel_id=1, source_target_pairs={{0,1},{1,4},{2,3},{3,6},{4,7},{5,2},{6,5},{7,0},{8,9},{9,10},{10,1... | collective-permute-start | bytes 24584 | tf_op jit(solution)/shard_map/ppermute | solution.py:284
  8.8 0.0 collective-permute-done.1.near
  8.8 0.0 copy-done
  8.8 0.0 copy-done.1
  8.8 0.0 copy-done.2
  8.8 0.0 copy-done.3
  8.8 1.4 %left.1 = (f32[2,34,8,288]{3,2,1,0:T(8,128)S(1)}, f32[2,8,128]{2,1,0:T(8,128)S(1)}, bf16[128,768]{1,0:T(8,128)(2,1)S(1)}, f32[144,128]{1,0:T(8,128)S(1)}, f32[5,576,128]{2,1,0:T(8,128)S(1)}) custom-call(f32[2,34,8,288]{3,2,1,0:T(8,128)S(1)} %get-tuple-element.17.fore, f32[2,34,8,288]{3,2,1,0:T(8,128)S(1)} %get-tuple-element.18.rear, ...), custom_call_target="tpu_custom_call" | custom-call | tf_op jit(solution)/shard_map/left/pallas_call | solution.py:302
  10.3 0.0 collective-permute-done.2.from_next
  10.3 1.5 %collective-permute-done.3.from_second = f32[8,256]{1,0:T(8,128)S(1)} collective-permute-done((f32[8,256]{1,0:T(8,128)S(1)}, f32[8,256]{1,0:T(8,128)S(1)}, u32[]{:S(2)}, u32[]{:S(2)}) %collective-permute-start.3) | collective-permute-done | bytes 8224 | tf_op jit(solution)/shard_map/ppermute | solution.py:296
  11.8 0.1 collective-permute-done.4.from_third
  11.9 1.2 %right.1 = (f32[544,288]{1,0:T(8,128)S(1)}, f32[5,144,128]{2,1,0:T(8,128)S(1)}) custom-call(f32[5,576,128]{2,1,0:T(8,128)S(1)} %get-tuple-element.21.z, bf16[128,768]{1,0:T(8,128)(2,1)S(1)} %get-tuple-element.22.chosen, f32[8,256]{1,0:T(8,128)S(1)} %get-tuple-element.19.mine, f32[8,256]{1,0:T(8,128)S(1)} %collective-permute-done.2.from_next, ...), custom_call_target="tpu_custom_call" | custom-call | tf_op jit(solution)/shard_map/right/pallas_call | solution.py:311
  13.1 2.2 %collective-permute-done.outer = f32[153,8,128]{2,1,0:T(8,128)S(1)} collective-permute-done((f32[153,8,128]{2,1,0:T(8,128)S(1)}, f32[153,8,128]{2,1,0:T(8,128)S(1)}, u32[]{:S(2)}, u32[]{:S(2)}) %collective-permute-start) | collective-permute-done | bytes 626720 | tf_op jit(solution)/shard_map/ppermute | solution.py:294
  15.3 2.7 %last.1 = f32[4,272,288]{2,1,0:T(8,128)} custom-call(f32[153,8,128]{2,1,0:T(8,128)S(1)} %collective-permute-done.outer, f32[2,34,8,288]{3,2,1,0:T(8,128)S(1)} %get-tuple-element.20.sums, f32[5,144,128]{2,1,0:T(8,128)S(1)} %get-tuple-element.23.pair_coef, f32[144,128]{1,0:T(8,128)S(1)} %get-tuple-element.24.atom_coef, ...), custom_call_target="tpu_custom_call" | custom-call | tf_op jit(solution)/shard_map/last/pallas_call | solution.py:320
Async XLA Ops:
  0.0 8.8 %copy-start = (s32[8,34]{1,0:T(8,128)S(1)}, s32[8,34]{1,0:T(8,128)}, u32[]{:S(2)}) copy-start(s32[8,34]{1,0:T(8,128)} %neighbours.1) | copy-start | bytes 3268
  0.0 8.8 %copy-start.1 = (s32[64]{0:T(128)S(1)}, s32[64]{0:T(128)}, u32[]{:S(2)}) copy-start(s32[64]{0:T(128)} %param.9) | copy-start | bytes 772
  0.0 8.8 %copy-start.2 = (f32[64]{0:T(128)S(1)}, f32[64]{0:T(128)}, u32[]{:S(2)}) copy-start(f32[64]{0:T(128)} %param.10) | copy-start | bytes 772
  0.0 8.8 %copy-start.3 = (f32[64]{0:T(128)S(1)}, f32[64]{0:T(128)}, u32[]{:S(2)}) copy-start(f32[64]{0:T(128)} %param.11) | copy-start | bytes 772
  1.5 7.3 %collective-permute-start.1 = (f32[2,34,8,288]{3,2,1,0:T(8,128)S(1)}, f32[2,34,8,288]{3,2,1,0:T(8,128)S(1)}, u32[]{:S(2)}, u32[]{:S(2)}) collective-permute-start(f32[2,34,8,288]{3,2,1,0:T(8,128)S(1)} %get-tuple-element.18.rear), channel_id=1, source_target_pairs={{0,4},{4,0},{8,12},{12,8},{16,20},{20,16},{24,28},{28,24},{32,36},... | collective-permute-start | bytes 1880072 | tf_op jit(solution)/shard_map/ppermute | solution.py:295
  2.3 13.0 %collective-permute-start = (f32[153,8,128]{2,1,0:T(8,128)S(1)}, f32[153,8,128]{2,1,0:T(8,128)S(1)}, u32[]{:S(2)}, u32[]{:S(2)}) collective-permute-start(f32[153,8,128]{2,1,0:T(8,128)S(1)} %get-tuple-element.16), channel_id=1, source_target_pairs={{0,3},{1,2},{2,1},{3,0},{4,8},{5,9},{6,10},{7,11},{8,4},{9,5},{10,... | collective-permute-start | bytes 1880072 | tf_op jit(solution)/shard_map/ppermute | solution.py:294
  5.0 5.2 %collective-permute-start.2 = (f32[8,256]{1,0:T(8,128)S(1)}, f32[8,256]{1,0:T(8,128)S(1)}, u32[]{:S(2)}, u32[]{:S(2)}) collective-permute-start(f32[8,256]{1,0:T(8,128)S(1)} %get-tuple-element.19.mine), channel_id=1, source_target_pairs={{0,5},{1,0},{2,7},{3,2},{4,3},{5,6},{6,1},{7,4},{8,11},{9,8},{10,9... | collective-permute-start | bytes 24584 | tf_op jit(solution)/shard_map/ppermute | solution.py:285
  7.8 4.0 %collective-permute-start.3 = (f32[8,256]{1,0:T(8,128)S(1)}, f32[8,256]{1,0:T(8,128)S(1)}, u32[]{:S(2)}, u32[]{:S(2)}) collective-permute-start(f32[8,256]{1,0:T(8,128)S(1)} %get-tuple-element.19.mine), channel_id=1, source_target_pairs={{0,2},{1,3},{2,0},{3,1},{4,6},{5,7},{6,4},{7,5},{8,10},{9,11},{10,... | collective-permute-start | bytes 24584 | tf_op jit(solution)/shard_map/ppermute | solution.py:296
  8.1 3.7 %collective-permute-start.4 = (f32[8,256]{1,0:T(8,128)S(1)}, f32[8,256]{1,0:T(8,128)S(1)}, u32[]{:S(2)}, u32[]{:S(2)}) collective-permute-start(f32[8,256]{1,0:T(8,128)S(1)} %get-tuple-element.19.mine), channel_id=1, source_target_pairs={{0,1},{1,4},{2,3},{3,6},{4,7},{5,2},{6,5},{7,0},{8,9},{9,10},{10,1... | collective-permute-start | bytes 24584 | tf_op jit(solution)/shard_map/ppermute | solution.py:284

commit v4 on v3

--- a/solution.py
+++ b/solution.py
@@ -32,28 +32,39 @@
         target = fore.at[row] if row < 2 else rear.at[row - 2]
         copies.append(pltpu.make_async_copy(green.at[energy_of(row, core)], target, sem.at[row]))
     copies.append(pltpu.make_async_copy(coupling, matrices, sem.at[ROWS]))
-    for place in (4, 0, 1, 2, 3):
+    for place in (0, 1, 4, 2, 3):
         copies[place].start()
-    copies[4].wait()
-    pieces = [matrices[orbital] for orbital in range(ORB)] + [jnp.zeros((ATOM, 2 * LANES - ORB * ORB), F32)]
-    flat[...] = jnp.concatenate(pieces, axis=-1)
     for row in range(2):
         copies[row].wait()
         outer[NBR * row : NBR * (row + 1)] = fore[row, :, :, 0:128]
         outer[NBR * (2 + row) : NBR * (3 + row)] = fore[row, :, :, 128:256]
     tails = [fore[part // 2, TAIL * (part % 2) : TAIL * (part % 2 + 1), :, 256:288] for part in range(4)]
     outer[4 * NBR : PACK] = jnp.concatenate(tails, axis=-1)
+    copies[4].wait()
+    pieces = [matrices[orbital] for orbital in range(ORB)] + [jnp.zeros((ATOM, 2 * LANES - ORB * ORB), F32)]
+    flat[...] = jnp.concatenate(pieces, axis=-1)
     copies[2].wait()
     copies[3].wait()
 
 
 def filled(tile):
     return min(LANES, 2 * ROW - LANES * tile)
+
+
+FOLD = TILES - 1
+SMALL = 2 * ROW - LANES * FOLD
 
 
 def turn_in(tile, natural, x):
     size = filled(tile)
     rows = slice(LANES * tile, LANES * tile + size)
+    if tile == FOLD:
+        middle = natural[rows, 128:256].T
+        x[tile, 0:128, 0:size] = natural[rows, 0:128].T
+        x[tile, 128:144, 0:size] = middle[0:16]
+        x[tile, 0:112, size : 2 * size] = middle[16:128]
+        x[tile, 112:144, size : 2 * size] = natural[rows, 256:288].T
+        return
     x[tile, 0:128, 0:size] = natural[rows, 0:128].T
     x[tile, 128:256, 0:size] = natural[rows, 128:256].T
     x[tile, 256:288, 0:size] = natural[rows, 256:288].T
@@ -62,6 +73,11 @@
 def turn_out(tile, result, y):
     size = filled(tile)
     rows = slice(LANES * tile, LANES * tile + size)
+    if tile == FOLD:
+        result[rows, 0:128] = y[tile, 0:128, 0:size].T
+        result[rows, 128:256] = jnp.concatenate([y[tile, 128:144, 0:size], y[tile, 0:112, size : 2 * size]], axis=0).T
+        result[rows, 256:288] = y[tile, 112:144, size : 2 * size].T
+        return
     result[rows, 0:128] = y[tile, 0:128, 0:size].T
     result[rows, 128:256] = y[tile, 128:256, 0:size].T
     result[rows, 256:288] = y[tile, 256:288, 0:size].T
@@ -73,15 +89,16 @@
 
 def left(tile, atom_coef, x, z):
     low = lax.broadcasted_iota(jnp.int32, (8, LANES), 0) < 4
+    parts = range(1 if tile == FOLD else 2)
     for block in range(0, ORB, 6):
         totals = {}
         for pair in range(6):
-            values = [[x[tile, pl.ds(144 * part + 24 * pair + 8 * k, 8)] for k in range(3)] for part in range(2)]
+            values = [[x[tile, pl.ds(144 * part + 24 * pair + 8 * k, 8)] for k in range(3)] for part in parts]
             for a in range(block, block + 6):
                 first = jnp.broadcast_to(atom_coef[ORB * a + 2 * pair : ORB * a + 2 * pair + 1], (8, LANES))
                 last = jnp.broadcast_to(atom_coef[ORB * a + 2 * pair + 1 : ORB * a + 2 * pair + 2], (8, LANES))
                 coef = (first, jnp.where(low, first, last), last)
-                for part in range(2):
+                for part in parts:
                     for k in range(3):
                         term = coef[k] * values[part][k]
                         totals[a, part, k] = term if pair == 0 else totals[a, part, k] + term
@@ -91,11 +108,12 @@
 
 def right(tile, pair_coef, z, y):
     totals = {}
+    groups = range(2 if tile == FOLD else 3)
     for d in range(ORB):
-        values = [z[tile, pl.ds(192 * k + d, 8, stride=24)] + z[tile, pl.ds(192 * k + 12 + d, 8, stride=24)] for k in range(3)]
+        values = [z[tile, pl.ds(192 * k + d, 8, stride=24)] + z[tile, pl.ds(192 * k + 12 + d, 8, stride=24)] for k in groups]
         for f in range(ORB):
             coef = jnp.broadcast_to(pair_coef[tile, ORB * f + d : ORB * f + d + 1], (8, LANES))
-            for k in range(3):
+            for k in groups:
                 term = coef * values[k]
                 totals[f, k] = term if d == 0 else totals[f, k] + term
     for (f, k), total in totals.items():
@@ -129,7 +147,8 @@
     indices[:, 0:NBR] = neighbours[...].astype(F32)
     width = TILES * LANES
     lane = lax.broadcasted_iota(jnp.int32, (LANES, width), 1)
-    within = lane - jnp.where(lane >= ROW, ROW, 0) - jnp.where(lane >= 2 * ROW, ROW, 0)
+    lane = lane - jnp.where(lane >= 2 * ROW, SMALL, 0)
+    within = lane - jnp.where(lane >= ROW, ROW, 0)
     picks = (lax.shift_right_logical(within, 3) == lax.broadcasted_iota(jnp.int32, (LANES, width), 0)).astype(F32).astype(BF16)
     spread = jnp.dot(indices[...].astype(BF16), picks, preferred_element_type=F32)
     lane8 = lax.broadcasted_iota(jnp.int32, (ATOM, width), 1) & 7
@@ -205,8 +224,6 @@
 def last_kernel(outer, sums, pair_coef, atom_coef, weights, done, out, natural, result, x, z, y, sem):
     core = lax.axis_index("energy") % 2
     finished = [pltpu.make_async_copy(done.at[pl.ds(ROW * half, ROW)], out.at[energy_of(2 + half, core)], sem.at[TILES + 1 + half]) for half in range(2)]
-    for copy in finished:
-        copy.start()
     near, far = weights[0], weights[1]
     near_part, far_part = near[:, 0:32], far[:, 0:32]
 
@@ -229,13 +246,19 @@
 
     copies, after = sender(result, out, 0, core, sem)
     prepare(0)
-    for tile in range(TILES):
-        if tile + 1 < TILES:
-            prepare(tile + 1)
+    for copy in finished:
+        copy.start()
+    prepare(1)
+    for tile in range(TILES):
         left(tile, atom_coef, x, z)
+        if tile > 0:
+            turn_out(tile - 1, result, y)
+            after(tile - 1)
+        if tile + 2 < TILES:
+            prepare(tile + 2)
         right(tile, pair_coef, z, y)
-        turn_out(tile, result, y)
-        after(tile)
+    turn_out(TILES - 1, result, y)
+    after(TILES - 1)
     for copy in finished + copies:
         copy.wait()
 

time: 18.1 us -> 18.1 us (level)
  no operation moved by 1% of the time
where the time goes in v4:
time: 18.1 us; the launch traced here: 18 us
  starting transfers between devices  7.29 us (40%)
  Pallas kernels  6.91 us (38%)
  waiting for transfers between devices  3.75 us (21%)
    ppermute x1, starting transfers between devices, planned(): far = lax.ppermute(outer, ('energy', 'atom'), pairs)  2.75 us
    ppermute x1, starting transfers between devices, planned(): first = lax.ppermute(mine, ('energy', 'atom'), down)  2.73 us
    pallas_call x1, Pallas kernels, planned(): pl.pallas_call(last_kernel, out_shape=rows, in_specs=[vmem] * 6, out_spec...  2.73 us
    ppermute x1, waiting for transfers between devices, planned(): far = lax.ppermute(outer, ('energy', 'atom'), pairs)  2.09 us
    ppermute x1, waiting for transfers between devices, planned(): lax.ppermute(mine, 'atom', [(a, (a + 2) % atoms) for a in range(atoms)])  1.57 us
    pallas_call x1, Pallas kernels, planned(): pl.pallas_call(pack_kernel, out_shape=(shape((PACK, 8, LANES)), shape((2,...  1.48 us
    pallas_call x1, Pallas kernels, planned(): pl.pallas_call(right_kernel, out_shape=(shape((2 * ROW, WIDTH)), shape((T...  1.35 us
    pallas_call x1, Pallas kernels, planned(): pl.pallas_call(left_kernel, out_shape=(shape((2, NBR, ATOM, WIDTH)), shap...  1.35 us
  transfers between devices with their start and end apart: 5, of which 3 were waited for; matrix products, arithmetic and copies ran while one was open for 0% of the time, Pallas kernels for 15%

profile of v4, /device:TPU:103, one launch (start us, length us, event | category | flops | bytes accessed | tf_op | source)
XLA Modules:
  0.0 18.0 jit_solution(17598986453525830390)
XLA Ops:
  0.0 0.0 copy-start
  0.0 0.0 copy-start.1
  0.0 0.0 copy-start.2
  0.0 0.0 copy-start.3
  0.0 1.5 %pack.1 = (f32[153,8,128]{2,1,0:T(8,128)S(1)}, f32[2,34,8,288]{3,2,1,0:T(8,128)S(1)}, f32[2,34,8,288]{3,2,1,0:T(8,128)S(1)}, f32[8,256]{1,0:T(8,128)S(1)}) custom-call(f32[4,34,8,288]{3,2,1,0:T(8,128)} %bitcast.11, f32[12,8,12]{2,1,0:T(8,128)} %bitcast.12), custom_call_target="tpu_custom_call" | custom-call | tf_op jit(solution)/shard_map/pack/pallas_call | solution.py:276
  1.5 0.8 %collective-permute-start.1 = (f32[2,34,8,288]{3,2,1,0:T(8,128)S(1)}, f32[2,34,8,288]{3,2,1,0:T(8,128)S(1)}, u32[]{:S(2)}, u32[]{:S(2)}) collective-permute-start(f32[2,34,8,288]{3,2,1,0:T(8,128)S(1)} %get-tuple-element.18.rear), channel_id=1, source_target_pairs={{0,4},{4,0},{8,12},{12,8},{16,20},{20,16},{24,28},{28,24},{32,36},... | collective-permute-start | bytes 1880072 | tf_op jit(solution)/shard_map/ppermute | solution.py:318
  2.3 2.7 %collective-permute-start = (f32[153,8,128]{2,1,0:T(8,128)S(1)}, f32[153,8,128]{2,1,0:T(8,128)S(1)}, u32[]{:S(2)}, u32[]{:S(2)}) collective-permute-start(f32[153,8,128]{2,1,0:T(8,128)S(1)} %get-tuple-element.16), channel_id=1, source_target_pairs={{0,3},{1,2},{2,1},{3,0},{4,8},{5,9},{6,10},{7,11},{8,4},{9,5},{10,... | collective-permute-start | bytes 1880072 | tf_op jit(solution)/shard_map/ppermute | solution.py:317
  5.0 2.7 %collective-permute-start.2 = (f32[8,256]{1,0:T(8,128)S(1)}, f32[8,256]{1,0:T(8,128)S(1)}, u32[]{:S(2)}, u32[]{:S(2)}) collective-permute-start(f32[8,256]{1,0:T(8,128)S(1)} %get-tuple-element.19.mine), channel_id=1, source_target_pairs={{0,5},{1,0},{2,7},{3,2},{4,3},{5,6},{6,1},{7,4},{8,11},{9,8},{10,9... | collective-permute-start | bytes 24584 | tf_op jit(solution)/shard_map/ppermute | solution.py:308
  7.8 0.3 %collective-permute-start.3 = (f32[8,256]{1,0:T(8,128)S(1)}, f32[8,256]{1,0:T(8,128)S(1)}, u32[]{:S(2)}, u32[]{:S(2)}) collective-permute-start(f32[8,256]{1,0:T(8,128)S(1)} %get-tuple-element.19.mine), channel_id=1, source_target_pairs={{0,2},{1,3},{2,0},{3,1},{4,6},{5,7},{6,4},{7,5},{8,10},{9,11},{10,... | collective-permute-start | bytes 24584 | tf_op jit(solution)/shard_map/ppermute | solution.py:319
  8.1 0.7 %collective-permute-start.4 = (f32[8,256]{1,0:T(8,128)S(1)}, f32[8,256]{1,0:T(8,128)S(1)}, u32[]{:S(2)}, u32[]{:S(2)}) collective-permute-start(f32[8,256]{1,0:T(8,128)S(1)} %get-tuple-element.19.mine), channel_id=1, source_target_pairs={{0,1},{1,4},{2,3},{3,6},{4,7},{5,2},{6,5},{7,0},{8,9},{9,10},{10,1... | collective-permute-start | bytes 24584 | tf_op jit(solution)/shard_map/ppermute | solution.py:307
  8.8 0.0 collective-permute-done.1.near
  8.8 0.0 copy-done
  8.8 0.0 copy-done.1
  8.8 0.0 copy-done.2
  8.8 0.0 copy-done.3
  8.8 1.3 %left.1 = (f32[2,34,8,288]{3,2,1,0:T(8,128)S(1)}, f32[2,8,128]{2,1,0:T(8,128)S(1)}, bf16[128,768]{1,0:T(8,128)(2,1)S(1)}, f32[144,128]{1,0:T(8,128)S(1)}, f32[5,576,128]{2,1,0:T(8,128)S(1)}) custom-call(f32[2,34,8,288]{3,2,1,0:T(8,128)S(1)} %get-tuple-element.17.fore, f32[2,34,8,288]{3,2,1,0:T(8,128)S(1)} %get-tuple-element.18.rear, ...), custom_call_target="tpu_custom_call" | custom-call | tf_op jit(solution)/shard_map/left/pallas_call | solution.py:325
  10.2 0.0 collective-permute-done.2.from_next
  10.2 1.6 %collective-permute-done.3.from_second = f32[8,256]{1,0:T(8,128)S(1)} collective-permute-done((f32[8,256]{1,0:T(8,128)S(1)}, f32[8,256]{1,0:T(8,128)S(1)}, u32[]{:S(2)}, u32[]{:S(2)}) %collective-permute-start.3) | collective-permute-done | bytes 8224 | tf_op jit(solution)/shard_map/ppermute | solution.py:319
  11.8 0.1 collective-permute-done.4.from_third
  11.9 1.3 %right.1 = (f32[544,288]{1,0:T(8,128)S(1)}, f32[5,144,128]{2,1,0:T(8,128)S(1)}) custom-call(f32[5,576,128]{2,1,0:T(8,128)S(1)} %get-tuple-element.21.z, bf16[128,768]{1,0:T(8,128)(2,1)S(1)} %get-tuple-element.22.chosen, f32[8,256]{1,0:T(8,128)S(1)} %get-tuple-element.19.mine, f32[8,256]{1,0:T(8,128)S(1)} %collective-permute-done.2.from_next, ...), custom_call_target="tpu_custom_call" | custom-call | tf_op jit(solution)/shard_map/right/pallas_call | solution.py:334
  13.2 2.1 %collective-permute-done.outer = f32[153,8,128]{2,1,0:T(8,128)S(1)} collective-permute-done((f32[153,8,128]{2,1,0:T(8,128)S(1)}, f32[153,8,128]{2,1,0:T(8,128)S(1)}, u32[]{:S(2)}, u32[]{:S(2)}) %collective-permute-start) | collective-permute-done | bytes 626720 | tf_op jit(solution)/shard_map/ppermute | solution.py:317
  15.3 2.7 %last.1 = f32[4,272,288]{2,1,0:T(8,128)} custom-call(f32[153,8,128]{2,1,0:T(8,128)S(1)} %collective-permute-done.outer, f32[2,34,8,288]{3,2,1,0:T(8,128)S(1)} %get-tuple-element.20.sums, f32[5,144,128]{2,1,0:T(8,128)S(1)} %get-tuple-element.23.pair_coef, f32[144,128]{1,0:T(8,128)S(1)} %get-tuple-element.24.atom_coef, ...), custom_call_target="tpu_custom_call" | custom-call | tf_op jit(solution)/shard_map/last/pallas_call | solution.py:343
Async XLA Ops:
  0.0 8.8 %copy-start = (s32[8,34]{1,0:T(8,128)S(1)}, s32[8,34]{1,0:T(8,128)}, u32[]{:S(2)}) copy-start(s32[8,34]{1,0:T(8,128)} %neighbours.1) | copy-start | bytes 3268
  0.0 8.8 %copy-start.1 = (s32[64]{0:T(128)S(1)}, s32[64]{0:T(128)}, u32[]{:S(2)}) copy-start(s32[64]{0:T(128)} %param.9) | copy-start | bytes 772
  0.0 8.8 %copy-start.2 = (f32[64]{0:T(128)S(1)}, f32[64]{0:T(128)}, u32[]{:S(2)}) copy-start(f32[64]{0:T(128)} %param.10) | copy-start | bytes 772
  0.0 8.8 %copy-start.3 = (f32[64]{0:T(128)S(1)}, f32[64]{0:T(128)}, u32[]{:S(2)}) copy-start(f32[64]{0:T(128)} %param.11) | copy-start | bytes 772
  1.5 7.3 %collective-permute-start.1 = (f32[2,34,8,288]{3,2,1,0:T(8,128)S(1)}, f32[2,34,8,288]{3,2,1,0:T(8,128)S(1)}, u32[]{:S(2)}, u32[]{:S(2)}) collective-permute-start(f32[2,34,8,288]{3,2,1,0:T(8,128)S(1)} %get-tuple-element.18.rear), channel_id=1, source_target_pairs={{0,4},{4,0},{8,12},{12,8},{16,20},{20,16},{24,28},{28,24},{32,36},... | collective-permute-start | bytes 1880072 | tf_op jit(solution)/shard_map/ppermute | solution.py:318
  2.3 13.0 %collective-permute-start = (f32[153,8,128]{2,1,0:T(8,128)S(1)}, f32[153,8,128]{2,1,0:T(8,128)S(1)}, u32[]{:S(2)}, u32[]{:S(2)}) collective-permute-start(f32[153,8,128]{2,1,0:T(8,128)S(1)} %get-tuple-element.16), channel_id=1, source_target_pairs={{0,3},{1,2},{2,1},{3,0},{4,8},{5,9},{6,10},{7,11},{8,4},{9,5},{10,... | collective-permute-start | bytes 1880072 | tf_op jit(solution)/shard_map/ppermute | solution.py:317
  5.0 5.2 %collective-permute-start.2 = (f32[8,256]{1,0:T(8,128)S(1)}, f32[8,256]{1,0:T(8,128)S(1)}, u32[]{:S(2)}, u32[]{:S(2)}) collective-permute-start(f32[8,256]{1,0:T(8,128)S(1)} %get-tuple-element.19.mine), channel_id=1, source_target_pairs={{0,5},{1,0},{2,7},{3,2},{4,3},{5,6},{6,1},{7,4},{8,11},{9,8},{10,9... | collective-permute-start | bytes 24584 | tf_op jit(solution)/shard_map/ppermute | solution.py:308
  7.8 4.0 %collective-permute-start.3 = (f32[8,256]{1,0:T(8,128)S(1)}, f32[8,256]{1,0:T(8,128)S(1)}, u32[]{:S(2)}, u32[]{:S(2)}) collective-permute-start(f32[8,256]{1,0:T(8,128)S(1)} %get-tuple-element.19.mine), channel_id=1, source_target_pairs={{0,2},{1,3},{2,0},{3,1},{4,6},{5,7},{6,4},{7,5},{8,10},{9,11},{10,... | collective-permute-start | bytes 24584 | tf_op jit(solution)/shard_map/ppermute | solution.py:319
  8.1 3.7 %collective-permute-start.4 = (f32[8,256]{1,0:T(8,128)S(1)}, f32[8,256]{1,0:T(8,128)S(1)}, u32[]{:S(2)}, u32[]{:S(2)}) collective-permute-start(f32[8,256]{1,0:T(8,128)S(1)} %get-tuple-element.19.mine), channel_id=1, source_target_pairs={{0,1},{1,4},{2,3},{3,6},{4,7},{5,2},{6,5},{7,0},{8,9},{9,10},{10,1... | collective-permute-start | bytes 24584 | tf_op jit(solution)/shard_map/ppermute | solution.py:307
